TPU v7x, 32 devices: a whole 2x2x4 slice. The times are simulated.
32 devices in a mesh: visit: 4 (over z), patch: 8 (over y, x, core).
Axes of the slice: x: 2, y: 2, z: 4, core: 2. Of those that a mesh axis runs over, the one named last changes fastest.
Arguments:
- warped_tiles: bfloat16 [1024, 256, 256], P(('visit', 'patch')), may hold values from -6 to 6
- tile_weights: bfloat16 [1024], P(('visit', 'patch')), may hold values from 1 to 9984
- kernel_taps: bfloat16 [1024, 2, 15], P(('visit', 'patch')), may hold values from -3 to 3
- patch_routes: int32 [1024, 1], P(('visit', 'patch')), may hold values from 0 to 7; in each aligned block of 32 rows (0 to 31, 32 to 63, ...) at most 8 rows name the same one
Outputs:
- difference: bfloat16 [1024, 256, 256], P(('visit', 'patch'))
- coadd_image: bfloat16 [8, 256, 256], P('patch')
Inputs may be any that keep to these rules, and one draw needn't show every extreme that they name: `patch_routes`: among the 32 rows of one device no patch is named more than 8 times, a bound that some block reaches; every patch is named by some row.
All inputs are finite; a program needn't handle non-finite values.
Results may differ from a plain program's by a relative error of at most 0.0046.
Values may be sent and summed in bfloat16 or wider, within the bound.
A program may use at most 128 MiB of HBM per device.

v0:
```python
import functools
import jax
import jax.numpy as jnp
from jax import lax
from jax.experimental import pallas as pl
from jax.experimental.pallas import tpu as pltpu
from jax.sharding import PartitionSpec as P


def sum_kernel(routes, weights, tiles, part, totals, acc):
    acc[...] = jnp.zeros_like(acc)
    scales = weights[...].astype(jnp.float32)
    for t in range(tiles.shape[0]):
        acc[routes[t]] += tiles[t].astype(jnp.float32) * scales[0:1, t : t + 1]
    part[...] = acc[...].astype(part.dtype)

    @pl.when(pl.program_id(0) == 0)
    def _():
        totals[...] = jnp.zeros_like(totals)
        for t in range(tiles.shape[0]):
            totals[routes[t]] += jnp.broadcast_to(scales[0:1, t : t + 1], totals.shape[1:])


def local_sums(tiles, weights, routes, patches, chunk, dtype):
    count, side, _ = tiles.shape
    return pl.pallas_call(
        sum_kernel,
        grid_spec=pltpu.PrefetchScalarGridSpec(
            num_scalar_prefetch=1,
            grid=(side // chunk,),
            in_specs=[
                pl.BlockSpec(weights.shape, lambda i, *_: (0, 0)),
                pl.BlockSpec((count, chunk, side), lambda i, *_: (0, i, 0)),
            ],
            out_specs=[
                pl.BlockSpec((patches, chunk, side), lambda i, *_: (0, i, 0)),
                pl.BlockSpec((patches, 8, 128), lambda i, *_: (0, 0, 0)),
            ],
            scratch_shapes=[pltpu.VMEM((patches, chunk, side), jnp.float32)],
        ),
        out_shape=[
            jax.ShapeDtypeStruct((patches, side, side), dtype),
            jax.ShapeDtypeStruct((patches, 8, 128), jnp.float32),
        ],
        name="local_sums",
    )(routes, weights, tiles)


def band(row):
    half = 128
    ring = pltpu.roll(jnp.broadcast_to(row, (half, half)), 0, 1, stride=1, stride_axis=0)
    gap = lax.broadcasted_iota(jnp.int32, (half, half), 1) - lax.broadcasted_iota(jnp.int32, (half, half), 0)
    zero = jnp.zeros_like(ring)
    near = jnp.where((gap < 64) & (gap > -64), ring, zero).astype(jnp.bfloat16)
    upper = jnp.where(gap <= -64, ring, zero).astype(jnp.bfloat16)
    lower = jnp.where(gap >= 64, ring, zero).astype(jnp.bfloat16)
    return jnp.concatenate(
        [jnp.concatenate([near, upper], axis=1), jnp.concatenate([lower, near], axis=1)], axis=0
    )


def match_kernel(kernel, routes, taps, tiles, coadd, out, own, rings):
    step = pl.program_id(0)
    group = tiles.shape[0]

    @pl.when(step == 0)
    def _():
        tap = lax.broadcasted_iota(jnp.int32, (2 * kernel, 128), 0)
        lane = lax.broadcasted_iota(jnp.int32, (2 * kernel, 128), 1)
        reach = kernel // 2
        gap = jnp.where(lane >= 64, lane - 128, lane)
        hots = (tap == gap + reach) & (tap < kernel), (tap == kernel + reach - gap) & (tap >= kernel)
        for side, hot in enumerate(hots):
            rings[side] = jnp.dot(
                taps[...], hot.astype(jnp.float32).astype(jnp.bfloat16), preferred_element_type=jnp.float32
            )
        own[0] = coadd[lax.axis_index("patch")]

    places = [step * group + g for g in range(group)]
    row_passes = [
        jnp.dot(
            band(rings[0, pl.ds(place, 1), :]), coadd[routes[place]], preferred_element_type=jnp.float32
        ).astype(jnp.bfloat16)
        for place in places
    ]
    for g, place in enumerate(places):
        template = jnp.dot(
            row_passes[g], band(rings[1, pl.ds(place, 1), :]), preferred_element_type=jnp.float32
        ).astype(jnp.bfloat16)
        out[g] = (tiles[g].astype(jnp.float32) - template.astype(jnp.float32)).astype(out.dtype)


def subtract(tiles, taps, routes, coadd, group):
    count, side, _ = tiles.shape
    kernel = taps.shape[2]
    flat = taps.reshape(count, 2 * kernel)
    return pl.pallas_call(
        functools.partial(match_kernel, kernel),
        grid_spec=pltpu.PrefetchScalarGridSpec(
            num_scalar_prefetch=1,
            grid=(count // group,),
            in_specs=[
                pl.BlockSpec(flat.shape, lambda i, *_: (0, 0)),
                pl.BlockSpec((group, side, side), lambda i, *_: (i, 0, 0)),
                pl.BlockSpec(coadd.shape, lambda i, *_: (0, 0, 0)),
            ],
            out_specs=[
                pl.BlockSpec((group, side, side), lambda i, *_: (i, 0, 0)),
                pl.BlockSpec((1, side, side), lambda i, *_: (0, 0, 0)),
            ],
            scratch_shapes=[pltpu.VMEM((2, count, 128), jnp.float32)],
        ),
        out_shape=[
            jax.ShapeDtypeStruct(tiles.shape, jnp.bfloat16),
            jax.ShapeDtypeStruct((1, side, side), jnp.bfloat16),
        ],
        name="subtract",
    )(routes, flat, tiles, coadd)


def merge_kernel(chips, visits, part, totals, coadd, half, chip_sum, inbox, lane_sum, lane_in, mine,
                 tot_in, tot_mid, tot_z, core_s, core_r, chip_s, chip_r, lane_s, lane_r,
                 back_s, back_r, fan_s, fan_r, pair_s, pair_r, tot_s, tot_r, totz_s, totz_r):
    v = lax.axis_index("visit")
    p = lax.axis_index("patch")
    k, c = p // 2, p % 2
    patches = 2 * chips
    side = part.shape[2]
    rows = side // visits
    sibling = 2 * k + 1 - c

    def span(r):
        return pl.ds(pl.multiple_of(r * rows, rows), rows)

    def remote(src, dst, send, recv, visit, patch):
        return pltpu.make_async_remote_copy(
            src_ref=src, dst_ref=dst, send_sem=send, recv_sem=recv,
            device_id=(visit, patch), device_id_type=pl.DeviceIdType.MESH)

    def chip_at(o):
        return lax.rem(k + o, chips)

    def visit_at(o):
        return lax.rem(v + o, visits)

    def loop(low, high, body):
        if (high - low) <= 4:
            for i in range(low, high):
                body(i)
        else:
            lax.fori_loop(low, high, lambda i, _: (body(i), 0)[1], 0)

    def core_copy(j, r):
        return remote(part.at[j, 1 - c, span(r)], half.at[j, span(r)], core_s.at[j, r], core_r.at[j, r], v, sibling)

    def chip_copy(j, slot, r):
        return remote(chip_sum.at[j, span(r)], inbox.at[slot, span(r)], chip_s.at[j, r], chip_r.at[slot, r], v, 2 * j + c)

    def lane_copy(u, slot):
        return remote(lane_sum.at[u], lane_in.at[slot], lane_s.at[u], lane_r.at[slot], u, p)

    def tot_copy(q, slot):
        return remote(totals.at[q], tot_in.at[slot], tot_s.at[q], tot_r.at[slot], v, q)

    def totz_copy(u, slot):
        return remote(tot_mid, tot_z.at[slot], totz_s.at[u], totz_r.at[slot], u, p)

    def back_copy(u, r):
        piece = coadd.at[p, span(r)]
        return remote(piece, piece, back_s.at[u], back_r.at[r], u, p)

    def fan_copy(j, slot, r):
        piece = coadd.at[2 * slot + c, span(r)]
        return remote(piece, piece, fan_s.at[j, r], fan_r.at[slot, r], v, 2 * j + c)

    def pair_copy(j, core, r):
        piece = coadd.at[2 * j + core, span(r)]
        return remote(piece, piece, pair_s.at[j, r], pair_r.at[j, r], v, sibling)

    barrier = pltpu.get_barrier_semaphore()

    def greet_patch(o):
        pl.semaphore_signal(barrier, inc=1, device_id=(v, lax.rem(p + o, patches)), device_id_type=pl.DeviceIdType.MESH)

    def greet_visit(o):
        pl.semaphore_signal(barrier, inc=1, device_id=(visit_at(o), p), device_id_type=pl.DeviceIdType.MESH)

    loop(1, patches, greet_patch)
    loop(1, visits, greet_visit)
    pl.semaphore_wait(barrier, patches - 1 + visits - 1)

    def start_core(i):
        r = visit_at(i + 1)
        loop(1, chips + 1, lambda o: core_copy(chip_at(o), r).start())

    loop(0, visits, start_core)

    def start_tot(o):
        tot_copy(lax.rem(p + o, patches), p).start()

    loop(1, patches, start_tot)

    def send_chips(i):
        r = visit_at(i + 1)

        def one(o):
            j = chip_at(o)
            core_copy(j, r).wait_recv()
            chip_sum[j, span(r)] = (
                part[j, c, span(r)].astype(jnp.float32) + half[j, span(r)].astype(jnp.float32)
            ).astype(jnp.bfloat16)
            chip_copy(j, k, r).start()

        loop(1, chips, one)

    loop(0, visits, send_chips)

    tot_mid[...] = totals[p]

    def add_tot(o):
        q = lax.rem(p + o, patches)
        tot_copy(q, q).wait_recv()
        tot_mid[...] += tot_in[q]

    loop(1, patches, add_tot)
    loop(1, visits, lambda o: totz_copy(visit_at(o), v).start())

    def gather(r):
        core_copy(k, r).wait_recv()
        mine[...] = part[k, c, span(r)].astype(jnp.float32) + half[k, span(r)].astype(jnp.float32)

        def one(o):
            j = chip_at(o)
            chip_copy(j, j, r).wait_recv()
            mine[...] += inbox[j, span(r)].astype(jnp.float32)

        loop(1, chips, one)

    def send_lane(i):
        r = visit_at(i)
        gather(r)
        lane_sum[r] = mine[...].astype(jnp.bfloat16)
        lane_copy(r, v).start()

    loop(1, visits, send_lane)
    gather(v)
    tot_z[v] = tot_mid[...]

    def add_lane(o):
        u = visit_at(o)
        lane_copy(u, u).wait_recv()
        mine[...] += lane_in[u].astype(jnp.float32)
        totz_copy(u, u).wait_recv()
        tot_z[v] += tot_z[u]

    loop(1, visits, add_lane)
    coadd[p, span(v)] = (mine[...] / tot_z[v][0:1, 0:1]).astype(jnp.bfloat16)

    loop(1, visits, lambda o: back_copy(visit_at(o), v).start())

    def fan_out(r):
        loop(1, chips, lambda o: fan_copy(chip_at(o), k, r).start())
        pair_copy(k, c, r).start()

    def forward(r):
        def one(o):
            j = chip_at(o)
            fan_copy(j, j, r).wait_recv()
            pair_copy(j, c, r).start()

        loop(1, chips, one)

    fan_out(v)

    def relay(i):
        r = visit_at(i)
        back_copy(r, r).wait_recv()
        fan_out(r)
        forward(visit_at(i - 1))

    loop(1, visits, relay)
    forward(visit_at(visits - 1))

    def finish(i):
        def one(o):
            j = chip_at(o)
            pair_copy(j, 1 - c, i).wait_recv()
            pair_copy(j, c, i).wait_send()
            core_copy(j, i).wait_send()

        def peer(o):
            j = chip_at(o)
            chip_copy(j, k, i).wait_send()
            fan_copy(j, k, i).wait_send()

        loop(0, chips, one)
        loop(1, chips, peer)

    loop(0, visits, finish)

    def finish_visit(o):
        u = visit_at(o)
        lane_copy(u, v).wait_send()
        totz_copy(u, v).wait_send()
        back_copy(u, v).wait_send()

    loop(1, visits, finish_visit)
    loop(1, patches, lambda o: tot_copy(lax.rem(p + o, patches), p).wait_send())


def merge(part, totals, patches, visits):
    side = part.shape[1]
    chips = patches // 2
    rows = side // visits
    dma = pltpu.SemaphoreType.DMA
    block = pl.BlockSpec(memory_space=pltpu.VMEM)
    pairs = [dma((chips, visits))] * 2
    return pl.pallas_call(
        functools.partial(merge_kernel, chips, visits),
        in_specs=[block, block],
        out_specs=block,
        out_shape=jax.ShapeDtypeStruct((patches, side, side), jnp.bfloat16),
        scratch_shapes=[
            pltpu.VMEM((chips, side, side), jnp.bfloat16),
            pltpu.VMEM((chips, side, side), jnp.bfloat16),
            pltpu.VMEM((chips, side, side), jnp.bfloat16),
            pltpu.VMEM((visits, rows, side), jnp.bfloat16),
            pltpu.VMEM((visits, rows, side), jnp.bfloat16),
            pltpu.VMEM((rows, side), jnp.float32),
            pltpu.VMEM((patches, 8, 128), jnp.float32),
            pltpu.VMEM((8, 128), jnp.float32),
            pltpu.VMEM((visits, 8, 128), jnp.float32),
        ] + pairs + pairs + [dma((visits,))] * 4 + pairs + pairs + [dma((patches,))] * 2 + [dma((visits,))] * 2,
        compiler_params=pltpu.CompilerParams(collective_id=0, has_side_effects=True),
        name="merge",
    )(part.reshape(chips, 2, side, side), totals)


def local(warped_tiles, tile_weights, kernel_taps, patch_routes):
    patches = lax.axis_size("patch")
    side = warped_tiles.shape[1]
    routes = patch_routes[:, 0]
    part, totals = local_sums(warped_tiles, tile_weights[None, :], routes, patches, 64, jnp.bfloat16)
    coadd = merge(part, totals, patches, lax.axis_size("visit"))
    return tuple(subtract(warped_tiles, kernel_taps, routes, coadd, 4))


def solution(mesh):
    in_specs = (
        P(("visit", "patch"), None, None),
        P(("visit", "patch")),
        P(("visit", "patch"), None, None),
        P(("visit", "patch"), None),
    )
    out_specs = (P(("visit", "patch"), None, None), P("patch", None, None))
    return jax.shard_map(local, mesh=mesh, in_specs=in_specs, out_specs=out_specs, check_vma=False)
```

profile of v0, /device:TPU:9, one launch (start us, length us, event | category | flops | bytes accessed | tf_op | source)
XLA Modules:
  0.0 48.3 jit_solution(11865223459227197975)
XLA Ops:
  0.6 0.8 %copy.9 = bf16[32,2,15]{2,1,0:T(2,128)(2,1)S(1)} copy(bf16[32,2,15]{0,1,2:T(2,128)(2,1)} %param.6) | data formatting | bytes 3840 | tf_op jit(solution)/shard_map/reshape | solution.py:96
  1.4 0.7 %reshape.12.taps = bf16[32,30]{1,0:T(8,128)(2,1)} reshape(bf16[32,2,15]{2,1,0:T(2,128)(2,1)S(1)} %copy.9) | data formatting | bytes 3840 | tf_op jit(solution)/shard_map/reshape | solution.py:96
  2.1 5.5 %local_sums.1 = (bf16[8,256,256]{2,1,0:T(8,128)(2,1)}, f32[8,8,128]{2,1,0:T(8,128)}) custom-call(s32[32]{0:T(128)} %bitcast.4, bf16[1,32]{1,0:T(2,128)(2,1)} %bitcast.6, bf16[32,256,256]{2,1,0:T(8,128)(2,1)} %tiles.3), custom_call_target="tpu_custom_call" | custom-call | tf_op jit(solution)/shard_map/local_sums/pallas_call | solution.py:26
  7.6 31.2 %merge.1.coadd = bf16[8,256,256]{2,1,0:T(8,128)(2,1)} custom-call(bf16[4,2,256,256]{3,2,1,0:T(8,128)(2,1)} %bitcast.3, f32[8,8,128]{2,1,0:T(8,128)} %get-tuple-element.5.totals), custom_call_target="tpu_custom_call" | custom-call | tf_op jit(solution)/shard_map/merge/pallas_call | solution.py:318
  38.9 9.4 %subtract.1 = (bf16[32,256,256]{2,1,0:T(8,128)(2,1)}, bf16[1,256,256]{2,1,0:T(8,128)(2,1)}) custom-call(s32[32]{0:T(128)} %bitcast.5, bf16[32,30]{1,0:T(8,128)(2,1)} %reshape.12.taps, bf16[32,256,256]{2,1,0:T(8,128)(2,1)} %tiles.3, bf16[8,256,256]{2,1,0:T(8,128)(2,1)} %merge.1.coadd), custom_call_target="tpu_custom_call" | custom-call | tf_op jit(solution)/shard_map/subtract/pallas_call | solution.py:97
where the time goes:
time: 48.7 us; the launch traced here: 48.3 us
  Pallas kernels  46.2 us (95%)
  local copies, waits for them, and re-layouts  1.48 us (3%)
  between operations  0.64 us (1%)
    pallas_call x1, Pallas kernels, merge(): pl.pallas_call(functools.partial(merge_kernel, chips, visits), in_specs=[...  31.2 us
    pallas_call x1, Pallas kernels, subtract(): pl.pallas_call(functools.partial(match_kernel, kernel), grid_spec=pltpu.P...  9.42 us
    pallas_call x1, Pallas kernels, local_sums(): pl.pallas_call(sum_kernel, grid_spec=pltpu.PrefetchScalarGridSpec(num_sca...  5.51 us
    reshape x2, local copies, waits for them, and re-layouts, subtract(): flat = taps.reshape(count, 2 * kernel)  1.48 us

commit v1 on v0

--- a/solution.py
+++ b/solution.py
@@ -65,15 +65,14 @@
 
     @pl.when(step == 0)
     def _():
-        tap = lax.broadcasted_iota(jnp.int32, (2 * kernel, 128), 0)
-        lane = lax.broadcasted_iota(jnp.int32, (2 * kernel, 128), 1)
+        tap = lax.broadcasted_iota(jnp.int32, (kernel, 128), 0)
+        lane = lax.broadcasted_iota(jnp.int32, (kernel, 128), 1)
         reach = kernel // 2
         gap = jnp.where(lane >= 64, lane - 128, lane)
-        hots = (tap == gap + reach) & (tap < kernel), (tap == kernel + reach - gap) & (tap >= kernel)
-        for side, hot in enumerate(hots):
-            rings[side] = jnp.dot(
-                taps[...], hot.astype(jnp.float32).astype(jnp.bfloat16), preferred_element_type=jnp.float32
-            )
+        for side, hot in enumerate((tap == reach + gap, tap == reach - gap)):
+            rings[side] = lax.dot_general(
+                taps[:, side, :], hot.astype(jnp.float32).astype(jnp.bfloat16), (((0,), (0,)), ((), ())),
+                preferred_element_type=jnp.float32)
         own[0] = coadd[lax.axis_index("patch")]
 
     places = [step * group + g for g in range(group)]
@@ -93,14 +92,14 @@
 def subtract(tiles, taps, routes, coadd, group):
     count, side, _ = tiles.shape
     kernel = taps.shape[2]
-    flat = taps.reshape(count, 2 * kernel)
+    flat = taps.transpose(2, 1, 0)
     return pl.pallas_call(
         functools.partial(match_kernel, kernel),
         grid_spec=pltpu.PrefetchScalarGridSpec(
             num_scalar_prefetch=1,
             grid=(count // group,),
             in_specs=[
-                pl.BlockSpec(flat.shape, lambda i, *_: (0, 0)),
+                pl.BlockSpec(flat.shape, lambda i, *_: (0, 0, 0)),
                 pl.BlockSpec((group, side, side), lambda i, *_: (i, 0, 0)),
                 pl.BlockSpec(coadd.shape, lambda i, *_: (0, 0, 0)),
             ],
@@ -114,6 +113,7 @@
             jax.ShapeDtypeStruct(tiles.shape, jnp.bfloat16),
             jax.ShapeDtypeStruct((1, side, side), jnp.bfloat16),
         ],
+        compiler_params=pltpu.CompilerParams(vmem_limit_bytes=24 << 20),
         name="subtract",
     )(routes, flat, tiles, coadd)
 
@@ -342,7 +342,7 @@
     routes = patch_routes[:, 0]
     part, totals = local_sums(warped_tiles, tile_weights[None, :], routes, patches, 64, jnp.bfloat16)
     coadd = merge(part, totals, patches, lax.axis_size("visit"))
-    return tuple(subtract(warped_tiles, kernel_taps, routes, coadd, 4))
+    return tuple(subtract(warped_tiles, kernel_taps, routes, coadd, 16))
 
 
 def solution(mesh):

time: 48.7 us -> 46.4 us (0.953)
  Pallas kernels: 46.2 us -> 41.9 us
  local copies, waits for them, and re-layouts: 1.48 us -> 3.42 us
    pallas_call x1, Pallas kernels: 9.42 us -> 5.03 us  [subtract(): pl.pallas_call(functools.partial(match_kernel, kernel), grid_spec=pltpu.P...]
    unnamed x0 -> x8, local copies, waits for them, and re-layouts: none -> 3.42 us
    reshape x2 -> x0, local copies, waits for them, and re-layouts: 1.48 us -> none  [subtract(): flat = taps.reshape(count, 2 * kernel)]
where the time goes in v1:
time: 46.4 us; the launch traced here: 46 us
  Pallas kernels  41.9 us (90%)
  local copies, waits for them, and re-layouts  3.42 us (7%)
  between operations  0.68 us (1%)
    pallas_call x1, Pallas kernels, merge(): pl.pallas_call(functools.partial(merge_kernel, chips, visits), in_specs=[...  31.3 us
    pallas_call x1, Pallas kernels, local_sums(): pl.pallas_call(sum_kernel, grid_spec=pltpu.PrefetchScalarGridSpec(num_sca...  5.63 us
    pallas_call x1, Pallas kernels, subtract(): pl.pallas_call(functools.partial(match_kernel, kernel), grid_spec=pltpu.P...  5.03 us
    unnamed x8, local copies, waits for them, and re-layouts  3.42 us

profile of v1, /device:TPU:9, one launch (start us, length us, event | category | flops | bytes accessed | tf_op | source)
XLA Modules:
  0.0 46.0 jit_solution(432727672748817978)
XLA Ops:
  0.6 0.0 copy-start.3
  0.6 0.0 copy-start.2
  0.7 5.6 %local_sums.1 = (bf16[8,256,256]{2,1,0:T(8,128)(2,1)}, f32[8,8,128]{2,1,0:T(8,128)}) custom-call(s32[32]{0:T(128)} %bitcast.5, bf16[1,32]{1,0:T(2,128)(2,1)} %bitcast.8, bf16[32,256,256]{2,1,0:T(8,128)(2,1)} %tiles.3), custom_call_target="tpu_custom_call" | custom-call | tf_op jit(solution)/shard_map/local_sums/pallas_call | solution.py:26
  6.3 31.3 %merge.1.coadd = bf16[8,256,256]{2,1,0:T(8,128)(2,1)} custom-call(bf16[4,2,256,256]{3,2,1,0:T(8,128)(2,1)} %bitcast.7, f32[8,8,128]{2,1,0:T(8,128)} %get-tuple-element.5.totals), custom_call_target="tpu_custom_call" | custom-call | tf_op jit(solution)/shard_map/merge/pallas_call | solution.py:318
  37.6 0.0 copy-done.3
  37.6 0.0 copy-done.2
  37.6 0.0 copy-start
  37.6 2.2 %copy-done = bf16[32,256,256]{2,1,0:T(8,128)(2,1)S(1)} copy-done((bf16[32,256,256]{2,1,0:T(8,128)(2,1)S(1)}, bf16[32,256,256]{2,1,0:T(8,128)(2,1)}, u32[]{:S(2)}) %copy-start) | copy-done | bytes 4194328
  39.8 0.0 copy-start.1
  39.8 1.2 %copy-done.1 = bf16[8,256,256]{2,1,0:T(8,128)(2,1)S(1)} copy-done((bf16[8,256,256]{2,1,0:T(8,128)(2,1)S(1)}, bf16[8,256,256]{2,1,0:T(8,128)(2,1)}, u32[]{:S(2)}) %copy-start.1) | copy-done | bytes 1048600
  41.0 5.0 %subtract.1 = (bf16[32,256,256]{2,1,0:T(8,128)(2,1)}, bf16[1,256,256]{2,1,0:T(8,128)(2,1)}) custom-call(s32[32]{0:T(128)S(1)} %bitcast.6, bf16[15,2,32]{2,1,0:T(2,128)(2,1)S(1)} %bitcast.4, bf16[32,256,256]{2,1,0:T(8,128)(2,1)S(1)} %copy-done, bf16[8,256,256]{2,1,0:T(8,128)(2,1)S(1)} %copy-done.1), custom_call_target="tpu_custom_call" | custom-call | tf_op jit(solution)/shard_map/subtract/pallas_call | solution.py:96
Async XLA Ops:
  0.6 36.9 %copy-start.3 = (s32[32,1]{0,1:T(1,128)S(1)}, s32[32,1]{0,1:T(1,128)}, u32[]{:S(2)}) copy-start(s32[32,1]{0,1:T(1,128)} %param.7) | copy-start | bytes 388
  0.6 36.9 %copy-start.2 = (bf16[32,2,15]{0,1,2:T(2,128)(2,1)S(1)}, bf16[32,2,15]{0,1,2:T(2,128)(2,1)}, u32[]{:S(2)}) copy-start(bf16[32,2,15]{0,1,2:T(2,128)(2,1)} %param.6) | copy-start | bytes 5764
  37.6 2.2 %copy-start = (bf16[32,256,256]{2,1,0:T(8,128)(2,1)S(1)}, bf16[32,256,256]{2,1,0:T(8,128)(2,1)}, u32[]{:S(2)}) copy-start(bf16[32,256,256]{2,1,0:T(8,128)(2,1)} %tiles.3) | copy-start | bytes 12582916
  39.8 1.2 %copy-start.1 = (bf16[8,256,256]{2,1,0:T(8,128)(2,1)S(1)}, bf16[8,256,256]{2,1,0:T(8,128)(2,1)}, u32[]{:S(2)}) copy-start(bf16[8,256,256]{2,1,0:T(8,128)(2,1)} %merge.1.coadd) | copy-start | bytes 3145732

commit v2 on v1

v2 whole, which is shorter than its diff:
```python
import functools
import jax
import jax.numpy as jnp
from jax import lax
from jax.experimental import pallas as pl
from jax.experimental.pallas import tpu as pltpu
from jax.sharding import PartitionSpec as P

GRAIN = 16


def flip(number, other, size):
    result, bit = 0, 1
    while bit < size:
        mine, its = lax.rem(lax.div(number, bit), 2), other // bit % 2 if isinstance(other, int) else lax.rem(lax.div(other, bit), 2)
        result = result + bit * (mine + its - 2 * mine * its)
        bit *= 2
    return result


def loop(low, high, body):
    if high - low <= 4:
        for i in range(low, high):
            body(i)
    else:
        lax.fori_loop(low, high, lambda i, _: (body(i), 0)[1], 0)


def coadd_kernel(chips, visits, routes_far, weights_far, tiles, out, routes, weights, tbuf, mix, give, keep, half, chip_sum, inbox, mine,
                 lane_sum, lane_in, tot, tot_core, tot_chip, tot_plane, tot_lane,
                 small_s, load_s, core_s, core_r, chip_s, chip_r, lane_s, lane_r, back_s, back_r, fan_s, fan_r,
                 pair_s, pair_r, totc_s, totc_r, totp_s, totp_r, totz_s, totz_r):
    v = lax.axis_index("visit")
    p = lax.axis_index("patch")
    k, c = lax.div(p, 2), lax.rem(p, 2)
    patches = 2 * chips
    count, side, _ = tiles.shape
    rows = side // visits
    steps = [visits - 1 - i for i in range(visits)]
    order = [flip(v, o, visits) for o in steps]
    sibling = (v, 2 * k + 1 - c)

    def span(r):
        return pl.ds(pl.multiple_of(r * rows, rows), rows)

    def chip_at(o):
        return flip(k, o, chips)

    def plane_at(o):
        return (v, 2 * chip_at(o) + c)

    def visit_at(o):
        return flip(v, o, visits)

    def remote(src, dst, send, recv, device):
        return pltpu.make_async_remote_copy(
            src_ref=src, dst_ref=dst, send_sem=send, recv_sem=recv,
            device_id=device, device_id_type=pl.DeviceIdType.MESH)

    def load(i):
        piece = span(order[i])
        return pltpu.make_async_copy(tiles.at[:, piece], tbuf.at[:, piece], load_s.at[i])

    def core_copy(i):
        piece = span(order[i])
        return remote(give.at[:, piece], half.at[:, piece], core_s.at[i], core_r.at[i], sibling)

    def chip_copy(o, i):
        piece = span(order[i])
        return remote(chip_sum.at[o - 1, piece], inbox.at[o - 1, piece], chip_s.at[o - 1, i], chip_r.at[o - 1, i], plane_at(o))

    def lane_copy(o):
        return remote(lane_sum.at[o - 1], lane_in.at[o - 1], lane_s.at[o - 1], lane_r.at[o - 1], (visit_at(o), p))

    def back_copy(o, r):
        piece = out.at[k, c, span(r)]
        return remote(piece, piece, back_s.at[o - 1], back_r.at[o - 1], (visit_at(o), p))

    def fan_copy(o, i, chip):
        piece = out.at[chip, c, span(order[i])]
        return remote(piece, piece, fan_s.at[o - 1, i], fan_r.at[o - 1, i], plane_at(o))

    def pair_copy(i, core):
        piece = out.at[:, core, span(order[i])]
        return remote(piece, piece, pair_s.at[i], pair_r.at[i], sibling)

    def tot_core_copy():
        return remote(tot, tot_core, totc_s, totc_r, sibling)

    def tot_plane_copy(o):
        return remote(tot_chip, tot_plane.at[o - 1], totp_s.at[o - 1], totp_r.at[o - 1], plane_at(o))

    def tot_lane_copy(o):
        return remote(tot_core, tot_lane.at[o - 1], totz_s.at[o - 1], totz_r.at[o - 1], (visit_at(o), p))

    barrier = pltpu.get_barrier_semaphore()

    def greet(device):
        pl.semaphore_signal(barrier, inc=1, device_id=device, device_id_type=pl.DeviceIdType.MESH)

    small = [pltpu.make_async_copy(routes_far, routes, small_s.at[0]),
             pltpu.make_async_copy(weights_far, weights, small_s.at[1])]
    for copy in small:
        copy.start()
    for i in range(visits):
        load(i).start()
    greet(sibling)
    loop(1, chips, lambda o: greet(plane_at(o)))
    loop(1, visits, lambda o: greet((visit_at(o), p)))

    line = lax.broadcasted_iota(jnp.int32, (patches * GRAIN, count), 0)
    slot = lax.div(line, GRAIN)
    patch = jnp.where(slot < chips, 2 * slot + 1 - c, 2 * (slot - chips) + c)
    for copy in small:
        copy.wait()
    scales = weights[...].astype(jnp.float32)
    routed = jnp.where(routes[...] == patch, scales, 0.0).astype(jnp.bfloat16)
    grains = lax.div(lax.broadcasted_iota(jnp.int32, (count, count * GRAIN), 1), GRAIN)
    widen = (grains == lax.broadcasted_iota(jnp.int32, (count, count * GRAIN), 0)).astype(jnp.float32).astype(jnp.bfloat16)
    wide = jnp.dot(routed, widen, preferred_element_type=jnp.float32)
    same = lax.rem(lax.broadcasted_iota(jnp.int32, wide.shape, 0), GRAIN) == lax.rem(
        lax.broadcasted_iota(jnp.int32, wide.shape, 1), GRAIN)
    mix[...] = jnp.where(same, wide, 0.0).astype(jnp.bfloat16)
    named = jnp.where(routes[...] == lax.broadcasted_iota(jnp.int32, (patches, count), 0), scales, 0.0)
    tot[...] = jnp.dot(named.astype(jnp.bfloat16), jnp.ones((count, 128), jnp.bfloat16), preferred_element_type=jnp.float32)

    def sums(i):
        load(i).wait()
        for b in range(rows // GRAIN):
            piece = pl.ds(pl.multiple_of(order[i] * rows + b * GRAIN, GRAIN), GRAIN)
            got = jnp.dot(mix[...], tbuf[:, piece, :].reshape(count * GRAIN, side), preferred_element_type=jnp.float32)
            got = got.reshape(2, chips, GRAIN, side)
            give[:, piece, :] = got[0].astype(jnp.bfloat16)
            keep[:, piece, :] = got[1]

    def send_chips(i):
        core_copy(i).wait_recv()
        piece = span(order[i])

        def one(o):
            j = chip_at(o)
            chip_sum[o - 1, piece, :] = (keep[j, piece, :] + half[j, piece, :].astype(jnp.float32)).astype(jnp.bfloat16)
            chip_copy(o, i).start()

        loop(1, chips, one)

    def gather(i):
        piece = span(order[i])
        mine[...] = keep[k, piece, :] + half[k, piece, :].astype(jnp.float32)

        def one(o):
            chip_copy(o, i).wait_recv()
            mine[...] += inbox[o - 1, piece, :].astype(jnp.float32)

        loop(1, chips, one)

    sums(0)
    pl.semaphore_wait(barrier, 1 + chips - 1 + visits - 1)
    core_copy(0).start()
    tot_core_copy().start()
    for i in range(1, visits):
        sums(i)
        core_copy(i).start()
        send_chips(i - 1)
    tot_core_copy().wait()
    tot_chip[...] = tot[...] + tot_core[...]
    send_chips(visits - 1)
    loop(1, chips, lambda o: tot_plane_copy(o).start())

    for i in range(visits - 1):
        gather(i)
        lane_sum[steps[i] - 1] = mine[...].astype(jnp.bfloat16)
        lane_copy(steps[i]).start()
        if i == 0:
            tot_core[...] = tot_chip[...]

            def add_plane(o):
                tot_plane_copy(o).wait_recv()
                tot_core[...] += tot_plane[o - 1]

            loop(1, chips, add_plane)
            loop(1, visits, lambda o: tot_lane_copy(o).start())
    gather(visits - 1)
    tot[...] = tot_core[...]

    def add_lane(i):
        o = visits - 1 - i
        lane_copy(o).wait_recv()
        mine[...] += lane_in[o - 1].astype(jnp.float32)
        tot_lane_copy(o).wait_recv()
        tot[...] += tot_lane[o - 1]

    loop(0, visits - 1, add_lane)
    out[k, c, span(v), :] = (mine[...] / tot[pl.ds(p, 1), :][0:1, 0:1]).astype(jnp.bfloat16)

    def fan_out(i):
        loop(1, chips, lambda o: fan_copy(o, i, k).start())

    def forward(i):
        loop(1, chips, lambda o: fan_copy(o, i, chip_at(o)).wait_recv())
        pair_copy(i, c).start()

    loop(1, visits, lambda o: back_copy(o, v).start())
    fan_out(visits - 1)
    for i in range(visits - 2, -1, -1):
        back_copy(steps[i], order[i]).wait_recv()
        fan_out(i)
        forward(i + 1)
    forward(0)

    for i in range(visits - 1, -1, -1):
        pair_copy(i, 1 - c).wait_recv()

    def finish(i):
        core_copy(i).wait_send()
        pair_copy(i, c).wait_send()

        def peer(o):
            chip_copy(o, i).wait_send()
            fan_copy(o, i, k).wait_send()

        loop(1, chips, peer)

    for i in range(visits):
        finish(i)

    def finish_visit(o):
        lane_copy(o).wait_send()
        back_copy(o, v).wait_send()
        tot_lane_copy(o).wait_send()

    loop(1, visits, finish_visit)
    loop(1, chips, lambda o: tot_plane_copy(o).wait_send())


def coadds(tiles, weights, routes, patches, visits):
    count, side, _ = tiles.shape
    chips = patches // 2
    rows = side // visits
    dma = pltpu.SemaphoreType.DMA
    block = pl.BlockSpec(memory_space=pltpu.VMEM)
    far = pl.BlockSpec(memory_space=pltpu.HBM)
    lane = max(visits - 1, 1)
    peer = max(chips - 1, 1)
    bf16, f32 = jnp.bfloat16, jnp.float32
    return pl.pallas_call(
        functools.partial(coadd_kernel, chips, visits),
        in_specs=[far, far, far],
        out_specs=block,
        out_shape=jax.ShapeDtypeStruct((chips, 2, side, side), bf16),
        scratch_shapes=[
            pltpu.VMEM(routes.shape, routes.dtype),
            pltpu.VMEM(weights.shape, weights.dtype),
            pltpu.VMEM((count, side, side), bf16),
            pltpu.VMEM((patches * GRAIN, count * GRAIN), bf16),
            pltpu.VMEM((chips, side, side), bf16),
            pltpu.VMEM((chips, side, side), f32),
            pltpu.VMEM((chips, side, side), bf16),
            pltpu.VMEM((peer, side, side), bf16),
            pltpu.VMEM((peer, side, side), bf16),
            pltpu.VMEM((rows, side), f32),
            pltpu.VMEM((lane, rows, side), bf16),
            pltpu.VMEM((lane, rows, side), bf16),
            pltpu.VMEM((patches, 128), f32),
            pltpu.VMEM((patches, 128), f32),
            pltpu.VMEM((patches, 128), f32),
            pltpu.VMEM((peer, patches, 128), f32),
            pltpu.VMEM((lane, patches, 128), f32),
            dma((2,)), dma((visits,)), dma((visits,)), dma((visits,)), dma((peer, visits)), dma((peer, visits)),
            dma((lane,)), dma((lane,)), dma((lane,)), dma((lane,)), dma((peer, visits)), dma((peer, visits)),
            dma((visits,)), dma((visits,)), dma, dma, dma((peer,)), dma((peer,)), dma((lane,)), dma((lane,)),
        ],
        compiler_params=pltpu.CompilerParams(collective_id=0, has_side_effects=True, vmem_limit_bytes=40 << 20),
        name="coadds",
    )(*(pltpu.with_memory_space_constraint(x, pltpu.HBM) for x in (routes, weights, tiles)))


def band(row):
    half = 128
    ring = pltpu.roll(jnp.broadcast_to(row, (half, half)), 0, 1, stride=1, stride_axis=0)
    gap = lax.broadcasted_iota(jnp.int32, (half, half), 1) - lax.broadcasted_iota(jnp.int32, (half, half), 0)
    zero = jnp.zeros_like(ring)
    near = jnp.where((gap < 64) & (gap > -64), ring, zero).astype(jnp.bfloat16)
    upper = jnp.where(gap <= -64, ring, zero).astype(jnp.bfloat16)
    lower = jnp.where(gap >= 64, ring, zero).astype(jnp.bfloat16)
    return jnp.concatenate(
        [jnp.concatenate([near, upper], axis=1), jnp.concatenate([lower, near], axis=1)], axis=0
    )


def match_kernel(kernel, routes, taps, tiles, coadd, out, own, rings):
    step = pl.program_id(0)
    group = tiles.shape[0]

    @pl.when(step == 0)
    def _():
        tap = lax.broadcasted_iota(jnp.int32, (kernel, 128), 0)
        lane = lax.broadcasted_iota(jnp.int32, (kernel, 128), 1)
        reach = kernel // 2
        gap = jnp.where(lane >= 64, lane - 128, lane)
        for side, hot in enumerate((tap == reach + gap, tap == reach - gap)):
            rings[side] = lax.dot_general(
                taps[:, side, :], hot.astype(jnp.float32).astype(jnp.bfloat16), (((0,), (0,)), ((), ())),
                preferred_element_type=jnp.float32)
        own[0] = coadd[lax.axis_index("patch")]

    places = [step * group + g for g in range(group)]
    row_passes = [
        jnp.dot(
            band(rings[0, pl.ds(place, 1), :]), coadd[routes[place]], preferred_element_type=jnp.float32
        ).astype(jnp.bfloat16)
        for place in places
    ]
    for g, place in enumerate(places):
        template = jnp.dot(
            row_passes[g], band(rings[1, pl.ds(place, 1), :]), preferred_element_type=jnp.float32
        ).astype(jnp.bfloat16)
        out[g] = (tiles[g].astype(jnp.float32) - template.astype(jnp.float32)).astype(out.dtype)


def subtract(tiles, taps, routes, coadd, group):
    count, side, _ = tiles.shape
    kernel = taps.shape[2]
    flat = taps.transpose(2, 1, 0)
    return pl.pallas_call(
        functools.partial(match_kernel, kernel),
        grid_spec=pltpu.PrefetchScalarGridSpec(
            num_scalar_prefetch=1,
            grid=(count // group,),
            in_specs=[
                pl.BlockSpec(flat.shape, lambda i, *_: (0, 0, 0)),
                pl.BlockSpec((group, side, side), lambda i, *_: (i, 0, 0)),
                pl.BlockSpec(coadd.shape, lambda i, *_: (0, 0, 0)),
            ],
            out_specs=[
                pl.BlockSpec((group, side, side), lambda i, *_: (i, 0, 0)),
                pl.BlockSpec((1, side, side), lambda i, *_: (0, 0, 0)),
            ],
            scratch_shapes=[pltpu.VMEM((2, count, 128), jnp.float32)],
        ),
        out_shape=[
            jax.ShapeDtypeStruct(tiles.shape, jnp.bfloat16),
            jax.ShapeDtypeStruct((1, side, side), jnp.bfloat16),
        ],
        compiler_params=pltpu.CompilerParams(vmem_limit_bytes=24 << 20),
        name="subtract",
    )(routes, flat, tiles, coadd)


def local(warped_tiles, tile_weights, kernel_taps, patch_routes):
    patches = lax.axis_size("patch")
    side = warped_tiles.shape[1]
    coadd = coadds(warped_tiles, tile_weights[None, :], patch_routes.T, patches, lax.axis_size("visit"))
    return tuple(subtract(warped_tiles, kernel_taps, patch_routes[:, 0], coadd.reshape(patches, side, side), 16))


def solution(mesh):
    in_specs = (
        P(("visit", "patch"), None, None),
        P(("visit", "patch")),
        P(("visit", "patch"), None, None),
        P(("visit", "patch"), None),
    )
    out_specs = (P(("visit", "patch"), None, None), P("patch", None, None))
    return jax.shard_map(local, mesh=mesh, in_specs=in_specs, out_specs=out_specs, check_vma=False)
```

time: 46.4 us -> 38.5 us (0.83)
  the two profiles are of different devices: /device:TPU:9 before, /device:TPU:0 now
where the time goes in v2:
time: 38.5 us; the launch traced here: 38.3 us
  Pallas kernels  37.6 us (98%)
  between operations  0.69 us (2%)
    pallas_call x1, Pallas kernels, coadds(): pl.pallas_call(functools.partial(coadd_kernel, chips, visits), in_specs=[...  32.7 us
    pallas_call x1, Pallas kernels, subtract(): pl.pallas_call(functools.partial(match_kernel, kernel), grid_spec=pltpu.P...  4.96 us

profile of v2, /device:TPU:0, one launch (start us, length us, event | category | flops | bytes accessed | tf_op | source)
XLA Modules:
  0.0 38.3 jit_solution(4856336306538218277)
XLA Ops:
  0.6 0.0 copy-start.2
  0.6 0.0 copy-start
  0.7 0.0 copy-start.1
  0.7 32.7 %coadds.1 = bf16[4,2,256,256]{3,2,1,0:T(8,128)(2,1)S(1)} custom-call(s32[1,32]{1,0:T(1,128)} %bitcast.7, bf16[1,32]{1,0:T(2,128)(2,1)} %bitcast.9, bf16[32,256,256]{2,1,0:T(8,128)(2,1)} %tiles.3), custom_call_target="tpu_custom_call" | custom-call | tf_op jit(solution)/shard_map/coadds/pallas_call | solution.py:246
  33.3 0.0 copy-done.2
  33.3 0.0 copy-done
  33.3 0.0 copy-done.1
  33.4 5.0 %subtract.1 = (bf16[32,256,256]{2,1,0:T(8,128)(2,1)}, bf16[1,256,256]{2,1,0:T(8,128)(2,1)}) custom-call(s32[32]{0:T(128)S(1)} %bitcast.8, bf16[15,2,32]{2,1,0:T(2,128)(2,1)S(1)} %bitcast.6, bf16[32,256,256]{2,1,0:T(8,128)(2,1)S(1)} %copy-done, bf16[8,256,256]{2,1,0:T(8,128)(2,1)S(1)} %bitcast.5), custom_call_target="tpu_custom_call" | custom-call | tf_op jit(solution)/shard_map/subtract/pallas_call | solution.py:325
Async XLA Ops:
  0.6 32.7 %copy-start.2 = (s32[32,1]{0,1:T(1,128)S(1)}, s32[32,1]{0,1:T(1,128)}, u32[]{:S(2)}) copy-start(s32[32,1]{0,1:T(1,128)} %param.7) | copy-start | bytes 388
  0.6 32.7 %copy-start = (bf16[32,256,256]{2,1,0:T(8,128)(2,1)S(1)}, bf16[32,256,256]{2,1,0:T(8,128)(2,1)}, u32[]{:S(2)}) copy-start(bf16[32,256,256]{2,1,0:T(8,128)(2,1)} %tiles.3) | copy-start | bytes 12582916
  0.7 32.7 %copy-start.1 = (bf16[32,2,15]{0,1,2:T(2,128)(2,1)S(1)}, bf16[32,2,15]{0,1,2:T(2,128)(2,1)}, u32[]{:S(2)}) copy-start(bf16[32,2,15]{0,1,2:T(2,128)(2,1)} %param.6) | copy-start | bytes 5764

commit v3 on v2

v3 whole, which is shorter than its diff:
```python
import functools
import jax
import jax.numpy as jnp
from jax import lax
from jax.experimental import pallas as pl
from jax.experimental.pallas import tpu as pltpu
from jax.sharding import PartitionSpec as P

GRAIN = 16
PARTS = 1


def flip(number, other, size):
    result, bit = 0, 1
    while bit < size:
        mine, its = lax.rem(lax.div(number, bit), 2), other // bit % 2 if isinstance(other, int) else lax.rem(lax.div(other, bit), 2)
        result = result + bit * (mine + its - 2 * mine * its)
        bit *= 2
    return result


def loop(low, high, body):
    if high - low <= 4:
        for i in range(low, high):
            body(i)
    else:
        lax.fori_loop(low, high, lambda i, _: (body(i), 0)[1], 0)


def coadd_kernel(chips, visits, parts, routes_far, weights_far, tiles, out, routes, weights, tbuf, mix, give, keep, half, chip_sum, inbox, mine, held,
                 lane_sum, lane_in, tot, tot_core, tot_chip, tot_plane, tot_lane,
                 small_s, load_s, core_s, core_r, chip_s, chip_r, lane_s, lane_r, back_s, back_r, fan_s, fan_r,
                 pair_s, pair_r, totc_s, totc_r, totp_s, totp_r, totz_s, totz_r):
    v = lax.axis_index("visit")
    p = lax.axis_index("patch")
    k, c = lax.div(p, 2), lax.rem(p, 2)
    patches = 2 * chips
    count, side, _ = tiles.shape
    rows = side // visits
    units = parts * visits
    sub = rows // parts
    steps = [visits - 1 - n % visits for n in range(units)]
    others = [flip(v, o, visits) for o in range(visits)]
    firsts = [others[steps[n]] * rows + n // visits * sub for n in range(units)]
    sibling = (v, 2 * k + 1 - c)

    def span(n):
        return pl.ds(pl.multiple_of(firsts[n], sub), sub)

    known = {}

    def chip_at(o):
        if not isinstance(o, int):
            return flip(k, o, chips)
        if o not in known:
            known[o] = flip(k, o, chips)
        return known[o]

    def plane_at(o):
        return (v, 2 * chip_at(o) + c)

    def visit_at(o):
        return others[o] if isinstance(o, int) else flip(v, o, visits)

    def remote(src, dst, send, recv, device):
        return pltpu.make_async_remote_copy(
            src_ref=src, dst_ref=dst, send_sem=send, recv_sem=recv,
            device_id=device, device_id_type=pl.DeviceIdType.MESH)

    def load(i):
        piece = span(i)
        return pltpu.make_async_copy(tiles.at[:, piece], tbuf.at[:, piece], load_s.at[i])

    def core_copy(i):
        piece = span(i)
        return remote(give.at[:, piece], half.at[:, piece], core_s.at[i], core_r.at[i], sibling)

    def chip_copy(o, i):
        piece = span(i)
        return remote(chip_sum.at[o - 1, piece], inbox.at[o - 1, piece], chip_s.at[o - 1, i], chip_r.at[o - 1, i], plane_at(o))

    def lane_copy(s, o):
        return remote(lane_sum.at[s, o - 1], lane_in.at[s, o - 1], lane_s.at[s, o - 1], lane_r.at[s, o - 1], (visit_at(o), p))

    def own_unit(s):
        return s * visits + visits - 1

    def back_copy(s, o, n):
        piece = out.at[k, c, span(n)]
        return remote(piece, piece, back_s.at[s, o - 1], back_r.at[s, o - 1], (visit_at(o), p))

    def fan_copy(o, i, chip):
        piece = out.at[chip, c, span(i)]
        return remote(piece, piece, fan_s.at[o - 1, i], fan_r.at[o - 1, i], plane_at(o))

    def pair_copy(i, core):
        piece = out.at[:, core, span(i)]
        return remote(piece, piece, pair_s.at[i], pair_r.at[i], sibling)

    def tot_core_copy():
        return remote(tot, tot_core, totc_s, totc_r, sibling)

    def tot_plane_copy(o):
        return remote(tot_chip, tot_plane.at[o - 1], totp_s.at[o - 1], totp_r.at[o - 1], plane_at(o))

    def tot_lane_copy(o):
        return remote(tot_core, tot_lane.at[o - 1], totz_s.at[o - 1], totz_r.at[o - 1], (visit_at(o), p))

    barrier = pltpu.get_barrier_semaphore()

    def greet(device):
        pl.semaphore_signal(barrier, inc=1, device_id=device, device_id_type=pl.DeviceIdType.MESH)

    small = [pltpu.make_async_copy(routes_far, routes, small_s.at[0]),
             pltpu.make_async_copy(weights_far, weights, small_s.at[1])]
    for copy in small:
        copy.start()
    for o in range(1, chips if chips <= 4 else 1):
        chip_at(o)
    for i in range(units):
        load(i).start()
    greet(sibling)
    loop(1, chips, lambda o: greet(plane_at(o)))
    loop(1, visits, lambda o: greet((visit_at(o), p)))

    line = lax.broadcasted_iota(jnp.int32, (patches * GRAIN, count), 0)
    slot = lax.div(line, GRAIN)
    patch = jnp.where(slot < chips, 2 * slot + 1 - c, 2 * (slot - chips) + c)
    for copy in small:
        copy.wait()
    scales = weights[...].astype(jnp.float32)
    routed = jnp.where(routes[...] == patch, scales, 0.0).astype(jnp.bfloat16)
    grains = lax.div(lax.broadcasted_iota(jnp.int32, (count, count * GRAIN), 1), GRAIN)
    widen = (grains == lax.broadcasted_iota(jnp.int32, (count, count * GRAIN), 0)).astype(jnp.float32).astype(jnp.bfloat16)
    wide = jnp.dot(routed, widen, preferred_element_type=jnp.float32)
    same = lax.rem(lax.broadcasted_iota(jnp.int32, wide.shape, 0), GRAIN) == lax.rem(
        lax.broadcasted_iota(jnp.int32, wide.shape, 1), GRAIN)
    mix[...] = jnp.where(same, wide, 0.0).astype(jnp.bfloat16)
    named = jnp.where(routes[...] == lax.broadcasted_iota(jnp.int32, (patches, count), 0), scales, 0.0)
    tot[...] = jnp.dot(named.astype(jnp.bfloat16), jnp.ones((count, 128), jnp.bfloat16), preferred_element_type=jnp.float32)

    def sums(i):
        load(i).wait()
        for b in range(sub // GRAIN):
            piece = pl.ds(pl.multiple_of(firsts[i] + b * GRAIN, GRAIN), GRAIN)
            got = jnp.dot(mix[...], tbuf[:, piece, :].reshape(count * GRAIN, side), preferred_element_type=jnp.float32)
            got = got.reshape(2, chips, GRAIN, side)
            give[:, piece, :] = got[0].astype(jnp.bfloat16)
            keep[:, piece, :] = got[1]

    def send_chips(i):
        core_copy(i).wait_recv()
        piece = span(i)

        def one(o):
            j = chip_at(o)
            chip_sum[o - 1, piece, :] = (keep[j, piece, :] + half[j, piece, :].astype(jnp.float32)).astype(jnp.bfloat16)
            chip_copy(o, i).start()

        loop(1, chips, one)

    def gather(i):
        piece = span(i)
        mine[...] = keep[k, piece, :] + half[k, piece, :].astype(jnp.float32)

        def one(o):
            chip_copy(o, i).wait_recv()
            mine[...] += inbox[o - 1, piece, :].astype(jnp.float32)

        loop(1, chips, one)

    sums(0)
    pl.semaphore_wait(barrier, 1 + chips - 1 + visits - 1)
    core_copy(0).start()
    tot_core_copy().start()
    for i in range(1, units):
        sums(i)
        core_copy(i).start()
        send_chips(i - 1)
    tot_core_copy().wait()
    tot_chip[...] = tot[...] + tot_core[...]
    send_chips(units - 1)
    loop(1, chips, lambda o: tot_plane_copy(o).start())

    def total_of_plane():
        tot_core[...] = tot_chip[...]

        def add_plane(o):
            tot_plane_copy(o).wait_recv()
            tot_core[...] += tot_plane[o - 1]

        loop(1, chips, add_plane)
        loop(1, visits, lambda o: tot_lane_copy(o).start())

    def total_of_lane():
        tot[...] = tot_core[...]

        def add_lane(o):
            tot_lane_copy(o).wait_recv()
            tot[...] += tot_lane[o - 1]

        loop(1, visits, add_lane)

    for n in range(units):
        s = n // visits
        gather(n)
        if steps[n]:
            lane_sum[s, steps[n] - 1] = mine[...].astype(jnp.bfloat16)
            lane_copy(s, steps[n]).start()
        else:
            held[s] = mine[...]
        if n == 0:
            total_of_plane()

    def fan_out(n):
        loop(1, chips, lambda o: fan_copy(o, n, k).start())

    def forward(n):
        loop(1, chips, lambda o: fan_copy(o, n, chip_at(o)).wait_recv())
        pair_copy(n, c).start()

    for s in range(parts):
        for o in range(visits - 1, 0, -1):
            lane_copy(s, o).wait_recv()
            held[s] += lane_in[s, o - 1].astype(jnp.float32)
        if s == 0:
            total_of_lane()
        own = own_unit(s)
        out[k, c, span(own), :] = (held[s] / tot[pl.ds(p, 1), :][0:1, 0:1]).astype(jnp.bfloat16)
        for o in range(1, visits):
            back_copy(s, o, own).start()
        fan_out(own)

    for s in range(parts):
        for o in range(1, visits):
            n = own_unit(s) - o
            back_copy(s, o, n).wait_recv()
            fan_out(n)
        forward(own_unit(s))
    for s in range(parts):
        for o in range(1, visits):
            forward(own_unit(s) - o)

    for n in range(units):
        pair_copy(n, 1 - c).wait_recv()

    for n in range(units):
        core_copy(n).wait_send()
        pair_copy(n, c).wait_send()

        def peer(o):
            chip_copy(o, n).wait_send()
            fan_copy(o, n, k).wait_send()

        loop(1, chips, peer)

    for s in range(parts):
        for o in range(1, visits):
            lane_copy(s, o).wait_send()
            back_copy(s, o, own_unit(s)).wait_send()
    loop(1, visits, lambda o: tot_lane_copy(o).wait_send())
    loop(1, chips, lambda o: tot_plane_copy(o).wait_send())


def coadds(tiles, weights, routes, patches, visits):
    count, side, _ = tiles.shape
    chips = patches // 2
    rows = side // visits
    parts = PARTS if rows % (PARTS * GRAIN) == 0 else 1
    units, sub = parts * visits, rows // parts
    dma = pltpu.SemaphoreType.DMA
    block = pl.BlockSpec(memory_space=pltpu.VMEM)
    far = pl.BlockSpec(memory_space=pltpu.HBM)
    lane = max(visits - 1, 1)
    peer = max(chips - 1, 1)
    bf16, f32 = jnp.bfloat16, jnp.float32
    return pl.pallas_call(
        functools.partial(coadd_kernel, chips, visits, parts),
        in_specs=[far, far, far],
        out_specs=block,
        out_shape=jax.ShapeDtypeStruct((chips, 2, side, side), bf16),
        scratch_shapes=[
            pltpu.VMEM(routes.shape, routes.dtype),
            pltpu.VMEM(weights.shape, weights.dtype),
            pltpu.VMEM((count, side, side), bf16),
            pltpu.VMEM((patches * GRAIN, count * GRAIN), bf16),
            pltpu.VMEM((chips, side, side), bf16),
            pltpu.VMEM((chips, side, side), f32),
            pltpu.VMEM((chips, side, side), bf16),
            pltpu.VMEM((peer, side, side), bf16),
            pltpu.VMEM((peer, side, side), bf16),
            pltpu.VMEM((sub, side), f32),
            pltpu.VMEM((parts, sub, side), f32),
            pltpu.VMEM((parts, lane, sub, side), bf16),
            pltpu.VMEM((parts, lane, sub, side), bf16),
            pltpu.VMEM((patches, 128), f32),
            pltpu.VMEM((patches, 128), f32),
            pltpu.VMEM((patches, 128), f32),
            pltpu.VMEM((peer, patches, 128), f32),
            pltpu.VMEM((lane, patches, 128), f32),
            dma((2,)), dma((units,)), dma((units,)), dma((units,)), dma((peer, units)), dma((peer, units)),
            dma((parts, lane)), dma((parts, lane)), dma((parts, lane)), dma((parts, lane)), dma((peer, units)), dma((peer, units)),
            dma((units,)), dma((units,)), dma, dma, dma((peer,)), dma((peer,)), dma((lane,)), dma((lane,)),
        ],
        compiler_params=pltpu.CompilerParams(collective_id=0, has_side_effects=True, vmem_limit_bytes=40 << 20),
        name="coadds",
    )(*(pltpu.with_memory_space_constraint(x, pltpu.HBM) for x in (routes, weights, tiles)))


def band(row):
    half = 128
    ring = pltpu.roll(jnp.broadcast_to(row, (half, half)), 0, 1, stride=1, stride_axis=0)
    gap = lax.broadcasted_iota(jnp.int32, (half, half), 1) - lax.broadcasted_iota(jnp.int32, (half, half), 0)
    zero = jnp.zeros_like(ring)
    near = jnp.where((gap < 64) & (gap > -64), ring, zero).astype(jnp.bfloat16)
    upper = jnp.where(gap <= -64, ring, zero).astype(jnp.bfloat16)
    lower = jnp.where(gap >= 64, ring, zero).astype(jnp.bfloat16)
    return jnp.concatenate(
        [jnp.concatenate([near, upper], axis=1), jnp.concatenate([lower, near], axis=1)], axis=0
    )


def match_kernel(kernel, group, routes, taps, tiles, coadd, out, own, rings, ready, sent, own_sent):
    count, side, _ = tiles.shape
    tap = lax.broadcasted_iota(jnp.int32, (kernel, 128), 0)
    lane = lax.broadcasted_iota(jnp.int32, (kernel, 128), 1)
    reach = kernel // 2
    gap = jnp.where(lane >= 64, lane - 128, lane)
    mine = pltpu.make_async_copy(coadd.at[lax.axis_index("patch")], own.at[0], own_sent)
    mine.start()
    for side_, hot in enumerate((tap == reach + gap, tap == reach - gap)):
        rings[side_] = lax.dot_general(
            taps[:, side_, :], hot.astype(jnp.float32).astype(jnp.bfloat16), (((0,), (0,)), ((), ())),
            preferred_element_type=jnp.float32)

    def send(g):
        piece = pl.ds(g * group, group)
        return pltpu.make_async_copy(ready.at[piece], out.at[piece], sent.at[g])

    def rows(g):
        return [
            jnp.dot(band(rings[0, place : place + 1, :]), coadd[routes[place]],
                    preferred_element_type=jnp.float32).astype(jnp.bfloat16)
            for place in range(g * group, (g + 1) * group)]

    passes = rows(0)
    for g in range(count // group):
        later = rows(g + 1) if False and g + 1 < count // group else None
        for i in range(group):
            place = g * group + i
            template = jnp.dot(passes[i], band(rings[1, place : place + 1, :]),
                               preferred_element_type=jnp.float32).astype(jnp.bfloat16)
            ready[place] = (tiles[place].astype(jnp.float32) - template.astype(jnp.float32)).astype(jnp.bfloat16)
        send(g).start()
        if g + 1 < count // group:
            passes = later if False else rows(g + 1)
    for g in range(count // group):
        send(g).wait()
    mine.wait()


def subtract(tiles, taps, routes, coadd, group):
    count, side, _ = tiles.shape
    kernel = taps.shape[2]
    block = pl.BlockSpec(memory_space=pltpu.VMEM)
    return pl.pallas_call(
        functools.partial(match_kernel, kernel, group),
        in_specs=[pl.BlockSpec(memory_space=pltpu.SMEM), block, block, block],
        out_specs=[pl.BlockSpec(memory_space=pltpu.HBM)] * 2,
        out_shape=[
            pltpu.HBM(tiles.shape, jnp.bfloat16),
            pltpu.HBM((1, side, side), jnp.bfloat16),
        ],
        scratch_shapes=[
            pltpu.VMEM((2, count, 128), jnp.float32),
            pltpu.VMEM(tiles.shape, jnp.bfloat16),
            pltpu.SemaphoreType.DMA((count // group,)),
            pltpu.SemaphoreType.DMA,
        ],
        compiler_params=pltpu.CompilerParams(vmem_limit_bytes=24 << 20),
        name="subtract",
    )(routes, taps.transpose(2, 1, 0), tiles, coadd)


def local(warped_tiles, tile_weights, kernel_taps, patch_routes):
    patches = lax.axis_size("patch")
    side = warped_tiles.shape[1]
    coadd = coadds(warped_tiles, tile_weights[None, :], patch_routes.T, patches, lax.axis_size("visit"))
    return tuple(subtract(warped_tiles, kernel_taps, patch_routes[:, 0], coadd.reshape(patches, side, side), 4))


def solution(mesh):
    in_specs = (
        P(("visit", "patch"), None, None),
        P(("visit", "patch")),
        P(("visit", "patch"), None, None),
        P(("visit", "patch"), None),
    )
    out_specs = (P(("visit", "patch"), None, None), P("patch", None, None))
    return jax.shard_map(local, mesh=mesh, in_specs=in_specs, out_specs=out_specs, check_vma=False)
```

time: 38.5 us -> 34.2 us (0.89)
  Pallas kernels: 37.6 us -> 33.3 us
    pallas_call x2, Pallas kernels: 37.6 us -> 33.3 us  [the longest x1 29.3 us: coadds(): pl.pallas_call(functools.partial(coadd_kernel, chips, visits, parts), in_...]
where the time goes in v3:
time: 34.2 us; the launch traced here: 34 us
  Pallas kernels  33.3 us (97%)
  between operations  0.69 us (2%)
    pallas_call x1, Pallas kernels, coadds(): pl.pallas_call(functools.partial(coadd_kernel, chips, visits, parts), in_...  29.3 us
    pallas_call x1, Pallas kernels, subtract(): pl.pallas_call(functools.partial(match_kernel, kernel, group), in_specs=[...  4.08 us

profile of v3, /device:TPU:0, one launch (start us, length us, event | category | flops | bytes accessed | tf_op | source)
XLA Modules:
  0.0 34.0 jit_solution(18415736974886566349)
XLA Ops:
  0.6 0.0 copy-start.2
  0.6 0.0 copy-start
  0.7 0.0 copy-start.1
  0.7 29.3 %coadds.1 = bf16[4,2,256,256]{3,2,1,0:T(8,128)(2,1)S(1)} custom-call(s32[1,32]{1,0:T(1,128)} %bitcast.7, bf16[1,32]{1,0:T(2,128)(2,1)} %bitcast.9, bf16[32,256,256]{2,1,0:T(8,128)(2,1)} %tiles.3), custom_call_target="tpu_custom_call" | custom-call | tf_op jit(solution)/shard_map/coadds/pallas_call | solution.py:277
  29.9 0.0 copy-done.2
  29.9 0.0 copy-done
  29.9 0.0 copy-done.1
  30.0 4.1 %subtract.1 = (bf16[32,256,256]{2,1,0:T(8,128)(2,1)}, bf16[1,256,256]{2,1,0:T(8,128)(2,1)}) custom-call(s32[32]{0:T(128)S(1)} %bitcast.8, bf16[15,2,32]{2,1,0:T(2,128)(2,1)S(1)} %bitcast.6, bf16[32,256,256]{2,1,0:T(8,128)(2,1)S(1)} %copy-done, bf16[8,256,256]{2,1,0:T(8,128)(2,1)S(1)} %bitcast.5), custom_call_target="tpu_custom_call" | custom-call | tf_op jit(solution)/shard_map/subtract/pallas_call | solution.py:366
Async XLA Ops:
  0.6 29.3 %copy-start.2 = (s32[32,1]{0,1:T(1,128)S(1)}, s32[32,1]{0,1:T(1,128)}, u32[]{:S(2)}) copy-start(s32[32,1]{0,1:T(1,128)} %param.7) | copy-start | bytes 388
  0.6 29.3 %copy-start = (bf16[32,256,256]{2,1,0:T(8,128)(2,1)S(1)}, bf16[32,256,256]{2,1,0:T(8,128)(2,1)}, u32[]{:S(2)}) copy-start(bf16[32,256,256]{2,1,0:T(8,128)(2,1)} %tiles.3) | copy-start | bytes 12582916
  0.7 29.3 %copy-start.1 = (bf16[32,2,15]{0,1,2:T(2,128)(2,1)S(1)}, bf16[32,2,15]{0,1,2:T(2,128)(2,1)}, u32[]{:S(2)}) copy-start(bf16[32,2,15]{0,1,2:T(2,128)(2,1)} %param.6) | copy-start | bytes 5764

commit v4 on v3

--- a/solution.py
+++ b/solution.py
@@ -8,6 +8,7 @@
 
 GRAIN = 16
 PARTS = 1
+WINDOW = 3
 
 
 def flip(number, other, size):
@@ -176,10 +177,12 @@
     for i in range(1, units):
         sums(i)
         core_copy(i).start()
-        send_chips(i - 1)
+        if i <= WINDOW:
+            send_chips(i - 1)
     tot_core_copy().wait()
     tot_chip[...] = tot[...] + tot_core[...]
-    send_chips(units - 1)
+    if units <= WINDOW:
+        send_chips(units - 1)
     loop(1, chips, lambda o: tot_plane_copy(o).start())
 
     def total_of_plane():
@@ -209,6 +212,8 @@
             lane_copy(s, steps[n]).start()
         else:
             held[s] = mine[...]
+        if n + WINDOW < units:
+            send_chips(n + WINDOW)
         if n == 0:
             total_of_plane()
 

time: 34.2 us -> 32.8 us (0.959)
  Pallas kernels: 33.3 us -> 31.9 us
    pallas_call x1, Pallas kernels: 29.3 us -> 27.8 us  [coadds(): pl.pallas_call(functools.partial(coadd_kernel, chips, visits, parts), in_...]
where the time goes in v4:
time: 32.8 us; the launch traced here: 32.6 us
  Pallas kernels  31.9 us (97%)
  between operations  0.69 us (2%)
    pallas_call x1, Pallas kernels, coadds(): pl.pallas_call(functools.partial(coadd_kernel, chips, visits, parts), in_...  27.8 us
    pallas_call x1, Pallas kernels, subtract(): pl.pallas_call(functools.partial(match_kernel, kernel, group), in_specs=[...  4.08 us

profile of v4, /device:TPU:0, one launch (start us, length us, event | category | flops | bytes accessed | tf_op | source)
XLA Modules:
  0.0 32.6 jit_solution(14300477968063977168)
XLA Ops:
  0.6 0.0 copy-start.2
  0.6 0.0 copy-start
  0.7 0.0 copy-start.1
  0.7 27.8 %coadds.1 = bf16[4,2,256,256]{3,2,1,0:T(8,128)(2,1)S(1)} custom-call(s32[1,32]{1,0:T(1,128)} %bitcast.7, bf16[1,32]{1,0:T(2,128)(2,1)} %bitcast.9, bf16[32,256,256]{2,1,0:T(8,128)(2,1)} %tiles.3), custom_call_target="tpu_custom_call" | custom-call | tf_op jit(solution)/shard_map/coadds/pallas_call | solution.py:282
  28.5 0.0 copy-done.2
  28.5 0.0 copy-done
  28.5 0.0 copy-done.1
  28.5 4.1 %subtract.1 = (bf16[32,256,256]{2,1,0:T(8,128)(2,1)}, bf16[1,256,256]{2,1,0:T(8,128)(2,1)}) custom-call(s32[32]{0:T(128)S(1)} %bitcast.8, bf16[15,2,32]{2,1,0:T(2,128)(2,1)S(1)} %bitcast.6, bf16[32,256,256]{2,1,0:T(8,128)(2,1)S(1)} %copy-done, bf16[8,256,256]{2,1,0:T(8,128)(2,1)S(1)} %bitcast.5), custom_call_target="tpu_custom_call" | custom-call | tf_op jit(solution)/shard_map/subtract/pallas_call | solution.py:371
Async XLA Ops:
  0.6 27.9 %copy-start.2 = (s32[32,1]{0,1:T(1,128)S(1)}, s32[32,1]{0,1:T(1,128)}, u32[]{:S(2)}) copy-start(s32[32,1]{0,1:T(1,128)} %param.7) | copy-start | bytes 388
  0.6 27.9 %copy-start = (bf16[32,256,256]{2,1,0:T(8,128)(2,1)S(1)}, bf16[32,256,256]{2,1,0:T(8,128)(2,1)}, u32[]{:S(2)}) copy-start(bf16[32,256,256]{2,1,0:T(8,128)(2,1)} %tiles.3) | copy-start | bytes 12582916
  0.7 27.9 %copy-start.1 = (bf16[32,2,15]{0,1,2:T(2,128)(2,1)S(1)}, bf16[32,2,15]{0,1,2:T(2,128)(2,1)}, u32[]{:S(2)}) copy-start(bf16[32,2,15]{0,1,2:T(2,128)(2,1)} %param.6) | copy-start | bytes 5764

commit v5 on v3

--- a/solution.py
+++ b/solution.py
@@ -7,7 +7,6 @@
 from jax.sharding import PartitionSpec as P
 
 GRAIN = 16
-PARTS = 1
 
 
 def flip(number, other, size):
@@ -27,9 +26,9 @@
         lax.fori_loop(low, high, lambda i, _: (body(i), 0)[1], 0)
 
 
-def coadd_kernel(chips, visits, parts, routes_far, weights_far, tiles, out, routes, weights, tbuf, mix, give, keep, half, chip_sum, inbox, mine, held,
+def coadd_kernel(chips, visits, routes_far, weights_far, tiles, out, routes, weights, tbuf, mix, give, keep, half, chip_sum, inbox, mine, near, near_in,
                  lane_sum, lane_in, tot, tot_core, tot_chip, tot_plane, tot_lane,
-                 small_s, load_s, core_s, core_r, chip_s, chip_r, lane_s, lane_r, back_s, back_r, fan_s, fan_r,
+                 small_s, load_s, core_s, core_r, chip_s, chip_r, near_s, near_r, lane_s, lane_r, back_s, back_r, fan_s, fan_r,
                  pair_s, pair_r, totc_s, totc_r, totp_s, totp_r, totz_s, totz_r):
     v = lax.axis_index("visit")
     p = lax.axis_index("patch")
@@ -37,15 +36,14 @@
     patches = 2 * chips
     count, side, _ = tiles.shape
     rows = side // visits
-    units = parts * visits
-    sub = rows // parts
-    steps = [visits - 1 - n % visits for n in range(units)]
+    steps = [1] + list(range(visits - 1, 1, -1)) + [0]
     others = [flip(v, o, visits) for o in range(visits)]
-    firsts = [others[steps[n]] * rows + n // visits * sub for n in range(units)]
+    units = range(visits)
+    own = visits - 1
     sibling = (v, 2 * k + 1 - c)
 
     def span(n):
-        return pl.ds(pl.multiple_of(firsts[n], sub), sub)
+        return pl.ds(pl.multiple_of(others[steps[n]] * rows, rows), rows)
 
     known = {}
 
@@ -79,15 +77,15 @@
         piece = span(i)
         return remote(chip_sum.at[o - 1, piece], inbox.at[o - 1, piece], chip_s.at[o - 1, i], chip_r.at[o - 1, i], plane_at(o))
 
-    def lane_copy(s, o):
-        return remote(lane_sum.at[s, o - 1], lane_in.at[s, o - 1], lane_s.at[s, o - 1], lane_r.at[s, o - 1], (visit_at(o), p))
-
-    def own_unit(s):
-        return s * visits + visits - 1
-
-    def back_copy(s, o, n):
+    def near_copy():
+        return remote(near, near_in, near_s, near_r, (others[1], p))
+
+    def lane_copy(o):
+        return remote(lane_sum.at[o - 2], lane_in.at[o - 2], lane_s.at[o - 2], lane_r.at[o - 2], (others[o], p))
+
+    def back_copy(o, n):
         piece = out.at[k, c, span(n)]
-        return remote(piece, piece, back_s.at[s, o - 1], back_r.at[s, o - 1], (visit_at(o), p))
+        return remote(piece, piece, back_s.at[o - 1], back_r.at[o - 1], (others[o], p))
 
     def fan_copy(o, i, chip):
         piece = out.at[chip, c, span(i)]
@@ -117,7 +115,7 @@
         copy.start()
     for o in range(1, chips if chips <= 4 else 1):
         chip_at(o)
-    for i in range(units):
+    for i in units:
         load(i).start()
     greet(sibling)
     loop(1, chips, lambda o: greet(plane_at(o)))
@@ -141,27 +139,40 @@
 
     def sums(i):
         load(i).wait()
-        for b in range(sub // GRAIN):
-            piece = pl.ds(pl.multiple_of(firsts[i] + b * GRAIN, GRAIN), GRAIN)
+        for b in range(rows // GRAIN):
+            piece = pl.ds(pl.multiple_of(others[steps[i]] * rows + b * GRAIN, GRAIN), GRAIN)
             got = jnp.dot(mix[...], tbuf[:, piece, :].reshape(count * GRAIN, side), preferred_element_type=jnp.float32)
             got = got.reshape(2, chips, GRAIN, side)
             give[:, piece, :] = got[0].astype(jnp.bfloat16)
             keep[:, piece, :] = got[1]
 
+    def whole(i, j):
+        total = keep[j, span(i), :] + half[j, span(i), :].astype(jnp.float32)
+        return total + near_in[j].astype(jnp.float32) if i == own else total
+
+    def send_near():
+        core_copy(0).wait_recv()
+
+        def one(j):
+            near[j] = whole(0, j).astype(jnp.bfloat16)
+
+        loop(0, chips, one)
+        near_copy().start()
+
     def send_chips(i):
         core_copy(i).wait_recv()
-        piece = span(i)
+        if i == own:
+            near_copy().wait_recv()
 
         def one(o):
-            j = chip_at(o)
-            chip_sum[o - 1, piece, :] = (keep[j, piece, :] + half[j, piece, :].astype(jnp.float32)).astype(jnp.bfloat16)
+            chip_sum[o - 1, span(i), :] = whole(i, chip_at(o)).astype(jnp.bfloat16)
             chip_copy(o, i).start()
 
         loop(1, chips, one)
 
     def gather(i):
         piece = span(i)
-        mine[...] = keep[k, piece, :] + half[k, piece, :].astype(jnp.float32)
+        mine[...] = whole(i, k)
 
         def one(o):
             chip_copy(o, i).wait_recv()
@@ -173,13 +184,15 @@
     pl.semaphore_wait(barrier, 1 + chips - 1 + visits - 1)
     core_copy(0).start()
     tot_core_copy().start()
-    for i in range(1, units):
+    for i in range(1, visits):
         sums(i)
         core_copy(i).start()
-        send_chips(i - 1)
+        if i == 1:
+            send_near()
+        else:
+            send_chips(i - 1)
     tot_core_copy().wait()
     tot_chip[...] = tot[...] + tot_core[...]
-    send_chips(units - 1)
     loop(1, chips, lambda o: tot_plane_copy(o).start())
 
     def total_of_plane():
@@ -201,16 +214,20 @@
 
         loop(1, visits, add_lane)
 
-    for n in range(units):
-        s = n // visits
+    for n in range(1, own):
+        if n == max(own - 1, 1):
+            send_chips(own)
         gather(n)
-        if steps[n]:
-            lane_sum[s, steps[n] - 1] = mine[...].astype(jnp.bfloat16)
-            lane_copy(s, steps[n]).start()
-        else:
-            held[s] = mine[...]
-        if n == 0:
+        lane_sum[steps[n] - 2] = mine[...].astype(jnp.bfloat16)
+        lane_copy(steps[n]).start()
+        if n == 1:
             total_of_plane()
+    gather(own)
+    total_of_lane()
+    for o in range(visits - 1, 1, -1):
+        lane_copy(o).wait_recv()
+        mine[...] += lane_in[o - 2].astype(jnp.float32)
+    out[k, c, span(own), :] = (mine[...] / tot[pl.ds(p, 1), :][0:1, 0:1]).astype(jnp.bfloat16)
 
     def fan_out(n):
         loop(1, chips, lambda o: fan_copy(o, n, k).start())
@@ -219,45 +236,34 @@
         loop(1, chips, lambda o: fan_copy(o, n, chip_at(o)).wait_recv())
         pair_copy(n, c).start()
 
-    for s in range(parts):
-        for o in range(visits - 1, 0, -1):
-            lane_copy(s, o).wait_recv()
-            held[s] += lane_in[s, o - 1].astype(jnp.float32)
-        if s == 0:
-            total_of_lane()
-        own = own_unit(s)
-        out[k, c, span(own), :] = (held[s] / tot[pl.ds(p, 1), :][0:1, 0:1]).astype(jnp.bfloat16)
-        for o in range(1, visits):
-            back_copy(s, o, own).start()
-        fan_out(own)
-
-    for s in range(parts):
-        for o in range(1, visits):
-            n = own_unit(s) - o
-            back_copy(s, o, n).wait_recv()
-            fan_out(n)
-        forward(own_unit(s))
-    for s in range(parts):
-        for o in range(1, visits):
-            forward(own_unit(s) - o)
-
-    for n in range(units):
+    back = [steps.index(o) for o in range(1, visits)]
+    for o in range(1, visits):
+        back_copy(o, own).start()
+    fan_out(own)
+    for o in range(1, visits):
+        back_copy(o, back[o - 1]).wait_recv()
+        fan_out(back[o - 1])
+    for n in [own] + back:
+        forward(n)
+
+    for n in units:
         pair_copy(n, 1 - c).wait_recv()
 
-    for n in range(units):
+    for n in units:
         core_copy(n).wait_send()
         pair_copy(n, c).wait_send()
 
         def peer(o):
-            chip_copy(o, n).wait_send()
+            if n:
+                chip_copy(o, n).wait_send()
             fan_copy(o, n, k).wait_send()
 
         loop(1, chips, peer)
-
-    for s in range(parts):
-        for o in range(1, visits):
-            lane_copy(s, o).wait_send()
-            back_copy(s, o, own_unit(s)).wait_send()
+    near_copy().wait_send()
+    for o in range(1, visits):
+        if o > 1:
+            lane_copy(o).wait_send()
+        back_copy(o, own).wait_send()
     loop(1, visits, lambda o: tot_lane_copy(o).wait_send())
     loop(1, chips, lambda o: tot_plane_copy(o).wait_send())
 
@@ -266,16 +272,14 @@
     count, side, _ = tiles.shape
     chips = patches // 2
     rows = side // visits
-    parts = PARTS if rows % (PARTS * GRAIN) == 0 else 1
-    units, sub = parts * visits, rows // parts
     dma = pltpu.SemaphoreType.DMA
     block = pl.BlockSpec(memory_space=pltpu.VMEM)
     far = pl.BlockSpec(memory_space=pltpu.HBM)
-    lane = max(visits - 1, 1)
+    lane = max(visits - 2, 1)
     peer = max(chips - 1, 1)
     bf16, f32 = jnp.bfloat16, jnp.float32
     return pl.pallas_call(
-        functools.partial(coadd_kernel, chips, visits, parts),
+        functools.partial(coadd_kernel, chips, visits),
         in_specs=[far, far, far],
         out_specs=block,
         out_shape=jax.ShapeDtypeStruct((chips, 2, side, side), bf16),
@@ -289,18 +293,19 @@
             pltpu.VMEM((chips, side, side), bf16),
             pltpu.VMEM((peer, side, side), bf16),
             pltpu.VMEM((peer, side, side), bf16),
-            pltpu.VMEM((sub, side), f32),
-            pltpu.VMEM((parts, sub, side), f32),
-            pltpu.VMEM((parts, lane, sub, side), bf16),
-            pltpu.VMEM((parts, lane, sub, side), bf16),
+            pltpu.VMEM((rows, side), f32),
+            pltpu.VMEM((chips, rows, side), bf16),
+            pltpu.VMEM((chips, rows, side), bf16),
+            pltpu.VMEM((lane, rows, side), bf16),
+            pltpu.VMEM((lane, rows, side), bf16),
             pltpu.VMEM((patches, 128), f32),
             pltpu.VMEM((patches, 128), f32),
             pltpu.VMEM((patches, 128), f32),
             pltpu.VMEM((peer, patches, 128), f32),
-            pltpu.VMEM((lane, patches, 128), f32),
-            dma((2,)), dma((units,)), dma((units,)), dma((units,)), dma((peer, units)), dma((peer, units)),
-            dma((parts, lane)), dma((parts, lane)), dma((parts, lane)), dma((parts, lane)), dma((peer, units)), dma((peer, units)),
-            dma((units,)), dma((units,)), dma, dma, dma((peer,)), dma((peer,)), dma((lane,)), dma((lane,)),
+            pltpu.VMEM((visits - 1, patches, 128), f32),
+            dma((2,)), dma((visits,)), dma((visits,)), dma((visits,)), dma((peer, visits)), dma((peer, visits)), dma, dma,
+            dma((lane,)), dma((lane,)), dma((visits - 1,)), dma((visits - 1,)), dma((peer, visits)), dma((peer, visits)),
+            dma((visits,)), dma((visits,)), dma, dma, dma((peer,)), dma((peer,)), dma((visits - 1,)), dma((visits - 1,)),
         ],
         compiler_params=pltpu.CompilerParams(collective_id=0, has_side_effects=True, vmem_limit_bytes=40 << 20),
         name="coadds",
@@ -350,7 +355,7 @@
             place = g * group + i
             template = jnp.dot(passes[i], band(rings[1, place : place + 1, :]),
                                preferred_element_type=jnp.float32).astype(jnp.bfloat16)
-            ready[place] = (tiles[place].astype(jnp.float32) - template.astype(jnp.float32)).astype(jnp.bfloat16)
+            ready[place] = tiles[place] - template
         send(g).start()
         if g + 1 < count // group:
             passes = later if False else rows(g + 1)

time: 34.2 us -> 32.2 us (0.942)
  Pallas kernels: 33.3 us -> 31.3 us
    pallas_call x1, Pallas kernels: 29.3 us -> 27.3 us  [coadds(): pl.pallas_call(functools.partial(coadd_kernel, chips, visits), in_specs=[...]
where the time goes in v5:
time: 32.2 us; the launch traced here: 32 us
  Pallas kernels  31.3 us (97%)
  between operations  0.69 us (2%)
    pallas_call x1, Pallas kernels, coadds(): pl.pallas_call(functools.partial(coadd_kernel, chips, visits), in_specs=[...  27.3 us
    pallas_call x1, Pallas kernels, subtract(): pl.pallas_call(functools.partial(match_kernel, kernel, group), in_specs=[...  4.02 us

profile of v5, /device:TPU:0, one launch (start us, length us, event | category | flops | bytes accessed | tf_op | source)
XLA Modules:
  0.0 32.0 jit_solution(193139359312173049)
XLA Ops:
  0.6 0.0 copy-start.2
  0.6 0.0 copy-start
  0.7 0.0 copy-start.1
  0.7 27.3 %coadds.1 = bf16[4,2,256,256]{3,2,1,0:T(8,128)(2,1)S(1)} custom-call(s32[1,32]{1,0:T(1,128)} %bitcast.7, bf16[1,32]{1,0:T(2,128)(2,1)} %bitcast.9, bf16[32,256,256]{2,1,0:T(8,128)(2,1)} %tiles.3), custom_call_target="tpu_custom_call" | custom-call | tf_op jit(solution)/shard_map/coadds/pallas_call | solution.py:281
  28.0 0.0 copy-done.2
  28.0 0.0 copy-done
  28.0 0.0 copy-done.1
  28.0 4.0 %subtract.1 = (bf16[32,256,256]{2,1,0:T(8,128)(2,1)}, bf16[1,256,256]{2,1,0:T(8,128)(2,1)}) custom-call(s32[32]{0:T(128)S(1)} %bitcast.8, bf16[15,2,32]{2,1,0:T(2,128)(2,1)S(1)} %bitcast.6, bf16[32,256,256]{2,1,0:T(8,128)(2,1)S(1)} %copy-done, bf16[8,256,256]{2,1,0:T(8,128)(2,1)S(1)} %bitcast.5), custom_call_target="tpu_custom_call" | custom-call | tf_op jit(solution)/shard_map/subtract/pallas_call | solution.py:371
Async XLA Ops:
  0.6 27.3 %copy-start.2 = (s32[32,1]{0,1:T(1,128)S(1)}, s32[32,1]{0,1:T(1,128)}, u32[]{:S(2)}) copy-start(s32[32,1]{0,1:T(1,128)} %param.7) | copy-start | bytes 388
  0.6 27.3 %copy-start = (bf16[32,256,256]{2,1,0:T(8,128)(2,1)S(1)}, bf16[32,256,256]{2,1,0:T(8,128)(2,1)}, u32[]{:S(2)}) copy-start(bf16[32,256,256]{2,1,0:T(8,128)(2,1)} %tiles.3) | copy-start | bytes 12582916
  0.7 27.3 %copy-start.1 = (bf16[32,2,15]{0,1,2:T(2,128)(2,1)S(1)}, bf16[32,2,15]{0,1,2:T(2,128)(2,1)}, u32[]{:S(2)}) copy-start(bf16[32,2,15]{0,1,2:T(2,128)(2,1)} %param.6) | copy-start | bytes 5764

commit v6 on v5

--- a/solution.py
+++ b/solution.py
@@ -36,7 +36,9 @@
     patches = 2 * chips
     count, side, _ = tiles.shape
     rows = side // visits
-    steps = [1] + list(range(visits - 1, 1, -1)) + [0]
+    steps = [visits - 1, 1] + list(range(visits - 2, 1, -1)) + [0]
+    first = steps.index(1)
+    farther = [n for n in range(visits) if steps[n] > 1]
     others = [flip(v, o, visits) for o in range(visits)]
     units = range(visits)
     own = visits - 1
@@ -121,21 +123,21 @@
     loop(1, chips, lambda o: greet(plane_at(o)))
     loop(1, visits, lambda o: greet((visit_at(o), p)))
 
-    line = lax.broadcasted_iota(jnp.int32, (patches * GRAIN, count), 0)
-    slot = lax.div(line, GRAIN)
+    slot = lax.shift_right_logical(lax.broadcasted_iota(jnp.int32, (patches * GRAIN, count), 0), 4)
     patch = jnp.where(slot < chips, 2 * slot + 1 - c, 2 * (slot - chips) + c)
+    grain = (count, count * GRAIN)
+    widen = (lax.shift_right_logical(lax.broadcasted_iota(jnp.int32, grain, 1), 4)
+             == lax.broadcasted_iota(jnp.int32, grain, 0)).astype(jnp.float32).astype(jnp.bfloat16)
+    grain = (GRAIN, count * GRAIN)
+    same = lax.broadcasted_iota(jnp.int32, grain, 0) == (lax.broadcasted_iota(jnp.int32, grain, 1) & (GRAIN - 1))
     for copy in small:
         copy.wait()
     scales = weights[...].astype(jnp.float32)
     routed = jnp.where(routes[...] == patch, scales, 0.0).astype(jnp.bfloat16)
-    grains = lax.div(lax.broadcasted_iota(jnp.int32, (count, count * GRAIN), 1), GRAIN)
-    widen = (grains == lax.broadcasted_iota(jnp.int32, (count, count * GRAIN), 0)).astype(jnp.float32).astype(jnp.bfloat16)
     wide = jnp.dot(routed, widen, preferred_element_type=jnp.float32)
-    same = lax.rem(lax.broadcasted_iota(jnp.int32, wide.shape, 0), GRAIN) == lax.rem(
-        lax.broadcasted_iota(jnp.int32, wide.shape, 1), GRAIN)
-    mix[...] = jnp.where(same, wide, 0.0).astype(jnp.bfloat16)
-    named = jnp.where(routes[...] == lax.broadcasted_iota(jnp.int32, (patches, count), 0), scales, 0.0)
-    tot[...] = jnp.dot(named.astype(jnp.bfloat16), jnp.ones((count, 128), jnp.bfloat16), preferred_element_type=jnp.float32)
+    for q in range(patches):
+        piece = slice(q * GRAIN, (q + 1) * GRAIN)
+        mix[piece, :] = jnp.where(same, wide[piece], 0.0).astype(jnp.bfloat16)
 
     def sums(i):
         load(i).wait()
@@ -151,10 +153,10 @@
         return total + near_in[j].astype(jnp.float32) if i == own else total
 
     def send_near():
-        core_copy(0).wait_recv()
+        core_copy(first).wait_recv()
 
         def one(j):
-            near[j] = whole(0, j).astype(jnp.bfloat16)
+            near[j] = whole(first, j).astype(jnp.bfloat16)
 
         loop(0, chips, one)
         near_copy().start()
@@ -183,45 +185,47 @@
     sums(0)
     pl.semaphore_wait(barrier, 1 + chips - 1 + visits - 1)
     core_copy(0).start()
+    named = jnp.where(routes[...] == lax.broadcasted_iota(jnp.int32, (patches, count), 0), scales, 0.0)
+    tot[...] = jnp.dot(named.astype(jnp.bfloat16), jnp.ones((count, 128), jnp.bfloat16), preferred_element_type=jnp.float32)
     tot_core_copy().start()
+    def total_of_plane():
+        tot_core[...] = tot_chip[...]
+
+        def add_plane(o):
+            tot_plane_copy(o).wait_recv()
+            tot_core[...] += tot_plane[o - 1]
+
+        loop(1, chips, add_plane)
+        loop(1, visits, lambda o: tot_lane_copy(o).start())
+
+    def total_of_lane():
+        tot[...] = tot_core[...]
+
+        def add_lane(o):
+            tot_lane_copy(o).wait_recv()
+            tot[...] += tot_lane[o - 1]
+
+        loop(1, visits, add_lane)
+
     for i in range(1, visits):
         sums(i)
         core_copy(i).start()
         if i == 1:
+            tot_core_copy().wait()
+            tot_chip[...] = tot[...] + tot_core[...]
+            loop(1, chips, lambda o: tot_plane_copy(o).start())
+        if i - 1 == first:
             send_near()
         else:
             send_chips(i - 1)
-    tot_core_copy().wait()
-    tot_chip[...] = tot[...] + tot_core[...]
-    loop(1, chips, lambda o: tot_plane_copy(o).start())
-
-    def total_of_plane():
-        tot_core[...] = tot_chip[...]
-
-        def add_plane(o):
-            tot_plane_copy(o).wait_recv()
-            tot_core[...] += tot_plane[o - 1]
-
-        loop(1, chips, add_plane)
-        loop(1, visits, lambda o: tot_lane_copy(o).start())
-
-    def total_of_lane():
-        tot[...] = tot_core[...]
-
-        def add_lane(o):
-            tot_lane_copy(o).wait_recv()
-            tot[...] += tot_lane[o - 1]
-
-        loop(1, visits, add_lane)
-
-    for n in range(1, own):
-        if n == max(own - 1, 1):
+
+    total_of_plane()
+    for n in farther:
+        if n == farther[-1]:
             send_chips(own)
         gather(n)
         lane_sum[steps[n] - 2] = mine[...].astype(jnp.bfloat16)
         lane_copy(steps[n]).start()
-        if n == 1:
-            total_of_plane()
     gather(own)
     total_of_lane()
     for o in range(visits - 1, 1, -1):
@@ -240,32 +244,30 @@
     for o in range(1, visits):
         back_copy(o, own).start()
     fan_out(own)
+    for n in units:
+        core_copy(n).wait_send()
+        if n != first:
+            loop(1, chips, lambda o: chip_copy(o, n).wait_send())
+    near_copy().wait_send()
+    for o in range(2, visits):
+        lane_copy(o).wait_send()
+    loop(1, visits, lambda o: tot_lane_copy(o).wait_send())
+    loop(1, chips, lambda o: tot_plane_copy(o).wait_send())
     for o in range(1, visits):
+        if o == visits - 1:
+            forward(own)
         back_copy(o, back[o - 1]).wait_recv()
         fan_out(back[o - 1])
-    for n in [own] + back:
+    for n in back:
         forward(n)
-
+    for o in range(1, visits):
+        back_copy(o, own).wait_send()
+    for n in units:
+        loop(1, chips, lambda o: fan_copy(o, n, k).wait_send())
+    for n in units:
+        pair_copy(n, c).wait_send()
     for n in units:
         pair_copy(n, 1 - c).wait_recv()
-
-    for n in units:
-        core_copy(n).wait_send()
-        pair_copy(n, c).wait_send()
-
-        def peer(o):
-            if n:
-                chip_copy(o, n).wait_send()
-            fan_copy(o, n, k).wait_send()
-
-        loop(1, chips, peer)
-    near_copy().wait_send()
-    for o in range(1, visits):
-        if o > 1:
-            lane_copy(o).wait_send()
-        back_copy(o, own).wait_send()
-    loop(1, visits, lambda o: tot_lane_copy(o).wait_send())
-    loop(1, chips, lambda o: tot_plane_copy(o).wait_send())
 
 
 def coadds(tiles, weights, routes, patches, visits):

time: 32.2 us -> 31.4 us (0.975)
  Pallas kernels: 31.3 us -> 30.6 us
    pallas_call x1, Pallas kernels: 27.3 us -> 26.6 us  [coadds(): pl.pallas_call(functools.partial(coadd_kernel, chips, visits), in_specs=[...]
where the time goes in v6:
time: 31.4 us; the launch traced here: 31.3 us
  Pallas kernels  30.6 us (97%)
  between operations  0.69 us (2%)
    pallas_call x1, Pallas kernels, coadds(): pl.pallas_call(functools.partial(coadd_kernel, chips, visits), in_specs=[...  26.6 us
    pallas_call x1, Pallas kernels, subtract(): pl.pallas_call(functools.partial(match_kernel, kernel, group), in_specs=[...  4.02 us

profile of v6, /device:TPU:0, one launch (start us, length us, event | category | flops | bytes accessed | tf_op | source)
XLA Modules:
  0.0 31.3 jit_solution(4924982411188323334)
XLA Ops:
  0.6 0.0 copy-start.2
  0.6 0.0 copy-start
  0.7 0.0 copy-start.1
  0.7 26.6 %coadds.1 = bf16[4,2,256,256]{3,2,1,0:T(8,128)(2,1)S(1)} custom-call(s32[1,32]{1,0:T(1,128)} %bitcast.7, bf16[1,32]{1,0:T(2,128)(2,1)} %bitcast.9, bf16[32,256,256]{2,1,0:T(8,128)(2,1)} %tiles.3), custom_call_target="tpu_custom_call" | custom-call | tf_op jit(solution)/shard_map/coadds/pallas_call | solution.py:283
  27.2 0.0 copy-done.2
  27.2 0.0 copy-done
  27.2 0.0 copy-done.1
  27.2 4.0 %subtract.1 = (bf16[32,256,256]{2,1,0:T(8,128)(2,1)}, bf16[1,256,256]{2,1,0:T(8,128)(2,1)}) custom-call(s32[32]{0:T(128)S(1)} %bitcast.8, bf16[15,2,32]{2,1,0:T(2,128)(2,1)S(1)} %bitcast.6, bf16[32,256,256]{2,1,0:T(8,128)(2,1)S(1)} %copy-done, bf16[8,256,256]{2,1,0:T(8,128)(2,1)S(1)} %bitcast.5), custom_call_target="tpu_custom_call" | custom-call | tf_op jit(solution)/shard_map/subtract/pallas_call | solution.py:373
Async XLA Ops:
  0.6 26.6 %copy-start.2 = (s32[32,1]{0,1:T(1,128)S(1)}, s32[32,1]{0,1:T(1,128)}, u32[]{:S(2)}) copy-start(s32[32,1]{0,1:T(1,128)} %param.7) | copy-start | bytes 388
  0.6 26.6 %copy-start = (bf16[32,256,256]{2,1,0:T(8,128)(2,1)S(1)}, bf16[32,256,256]{2,1,0:T(8,128)(2,1)}, u32[]{:S(2)}) copy-start(bf16[32,256,256]{2,1,0:T(8,128)(2,1)} %tiles.3) | copy-start | bytes 12582916
  0.7 26.6 %copy-start.1 = (bf16[32,2,15]{0,1,2:T(2,128)(2,1)S(1)}, bf16[32,2,15]{0,1,2:T(2,128)(2,1)}, u32[]{:S(2)}) copy-start(bf16[32,2,15]{0,1,2:T(2,128)(2,1)} %param.6) | copy-start | bytes 5764

commit v7 on v6

--- a/solution.py
+++ b/solution.py
@@ -79,8 +79,9 @@
         piece = span(i)
         return remote(chip_sum.at[o - 1, piece], inbox.at[o - 1, piece], chip_s.at[o - 1, i], chip_r.at[o - 1, i], plane_at(o))
 
-    def near_copy():
-        return remote(near, near_in, near_s, near_r, (others[1], p))
+    def near_copy(part):
+        piece = pl.ds(0, 1) if part else pl.ds(1, chips - 1)
+        return remote(near.at[piece], near_in.at[piece], near_s.at[part], near_r.at[part], (others[1], p))
 
     def lane_copy(o):
         return remote(lane_sum.at[o - 2], lane_in.at[o - 2], lane_s.at[o - 2], lane_r.at[o - 2], (others[o], p))
@@ -115,7 +116,7 @@
              pltpu.make_async_copy(weights_far, weights, small_s.at[1])]
     for copy in small:
         copy.start()
-    for o in range(1, chips if chips <= 4 else 1):
+    for o in range(chips if chips <= 4 else 1):
         chip_at(o)
     for i in units:
         load(i).start()
@@ -148,33 +149,38 @@
             give[:, piece, :] = got[0].astype(jnp.bfloat16)
             keep[:, piece, :] = got[1]
 
-    def whole(i, j):
+    def whole(i, o):
+        j = chip_at(o)
         total = keep[j, span(i), :] + half[j, span(i), :].astype(jnp.float32)
-        return total + near_in[j].astype(jnp.float32) if i == own else total
+        return total + near_in[o].astype(jnp.float32) if i == own else total
 
     def send_near():
         core_copy(first).wait_recv()
 
-        def one(j):
-            near[j] = whole(first, j).astype(jnp.bfloat16)
-
-        loop(0, chips, one)
-        near_copy().start()
+        def one(o):
+            near[o] = whole(first, o).astype(jnp.bfloat16)
+
+        loop(1, chips, one)
+        near_copy(0).start()
+        one(0)
+        near_copy(1).start()
 
     def send_chips(i):
         core_copy(i).wait_recv()
         if i == own:
-            near_copy().wait_recv()
+            near_copy(0).wait_recv()
 
         def one(o):
-            chip_sum[o - 1, span(i), :] = whole(i, chip_at(o)).astype(jnp.bfloat16)
+            chip_sum[o - 1, span(i), :] = whole(i, o).astype(jnp.bfloat16)
             chip_copy(o, i).start()
 
         loop(1, chips, one)
 
     def gather(i):
         piece = span(i)
-        mine[...] = whole(i, k)
+        if i == own:
+            near_copy(1).wait_recv()
+        mine[...] = whole(i, 0)
 
         def one(o):
             chip_copy(o, i).wait_recv()
@@ -248,7 +254,8 @@
         core_copy(n).wait_send()
         if n != first:
             loop(1, chips, lambda o: chip_copy(o, n).wait_send())
-    near_copy().wait_send()
+    near_copy(0).wait_send()
+    near_copy(1).wait_send()
     for o in range(2, visits):
         lane_copy(o).wait_send()
     loop(1, visits, lambda o: tot_lane_copy(o).wait_send())
@@ -305,7 +312,7 @@
             pltpu.VMEM((patches, 128), f32),
             pltpu.VMEM((peer, patches, 128), f32),
             pltpu.VMEM((visits - 1, patches, 128), f32),
-            dma((2,)), dma((visits,)), dma((visits,)), dma((visits,)), dma((peer, visits)), dma((peer, visits)), dma, dma,
+            dma((2,)), dma((visits,)), dma((visits,)), dma((visits,)), dma((peer, visits)), dma((peer, visits)), dma((2,)), dma((2,)),
             dma((lane,)), dma((lane,)), dma((visits - 1,)), dma((visits - 1,)), dma((peer, visits)), dma((peer, visits)),
             dma((visits,)), dma((visits,)), dma, dma, dma((peer,)), dma((peer,)), dma((visits - 1,)), dma((visits - 1,)),
         ],

time: 31.4 us -> 31.3 us (level)
  no operation moved by 1% of the time
where the time goes in v7:
time: 31.3 us; the launch traced here: 31.1 us
  Pallas kernels  30.4 us (97%)
  between operations  0.69 us (2%)
    pallas_call x1, Pallas kernels, coadds(): pl.pallas_call(functools.partial(coadd_kernel, chips, visits), in_specs=[...  26.4 us
    pallas_call x1, Pallas kernels, subtract(): pl.pallas_call(functools.partial(match_kernel, kernel, group), in_specs=[...  4.03 us

profile of v7, /device:TPU:0, one launch (start us, length us, event | category | flops | bytes accessed | tf_op | source)
XLA Modules:
  0.0 31.1 jit_solution(3291816627953373833)
XLA Ops:
  0.6 0.0 copy-start.2
  0.6 0.0 copy-start
  0.7 0.0 copy-start.1
  0.7 26.4 %coadds.1 = bf16[4,2,256,256]{3,2,1,0:T(8,128)(2,1)S(1)} custom-call(s32[1,32]{1,0:T(1,128)} %bitcast.7, bf16[1,32]{1,0:T(2,128)(2,1)} %bitcast.9, bf16[32,256,256]{2,1,0:T(8,128)(2,1)} %tiles.3), custom_call_target="tpu_custom_call" | custom-call | tf_op jit(solution)/shard_map/coadds/pallas_call | solution.py:290
  27.0 0.0 copy-done.2
  27.1 0.0 copy-done
  27.1 0.0 copy-done.1
  27.1 4.0 %subtract.1 = (bf16[32,256,256]{2,1,0:T(8,128)(2,1)}, bf16[1,256,256]{2,1,0:T(8,128)(2,1)}) custom-call(s32[32]{0:T(128)S(1)} %bitcast.8, bf16[15,2,32]{2,1,0:T(2,128)(2,1)S(1)} %bitcast.6, bf16[32,256,256]{2,1,0:T(8,128)(2,1)S(1)} %copy-done, bf16[8,256,256]{2,1,0:T(8,128)(2,1)S(1)} %bitcast.5), custom_call_target="tpu_custom_call" | custom-call | tf_op jit(solution)/shard_map/subtract/pallas_call | solution.py:380
Async XLA Ops:
  0.6 26.4 %copy-start.2 = (s32[32,1]{0,1:T(1,128)S(1)}, s32[32,1]{0,1:T(1,128)}, u32[]{:S(2)}) copy-start(s32[32,1]{0,1:T(1,128)} %param.7) | copy-start | bytes 388
  0.6 26.4 %copy-start = (bf16[32,256,256]{2,1,0:T(8,128)(2,1)S(1)}, bf16[32,256,256]{2,1,0:T(8,128)(2,1)}, u32[]{:S(2)}) copy-start(bf16[32,256,256]{2,1,0:T(8,128)(2,1)} %tiles.3) | copy-start | bytes 12582916
  0.7 26.4 %copy-start.1 = (bf16[32,2,15]{0,1,2:T(2,128)(2,1)S(1)}, bf16[32,2,15]{0,1,2:T(2,128)(2,1)}, u32[]{:S(2)}) copy-start(bf16[32,2,15]{0,1,2:T(2,128)(2,1)} %param.6) | copy-start | bytes 5764

commit v8 on v7

--- a/solution.py
+++ b/solution.py
@@ -247,7 +247,7 @@
         pair_copy(n, c).start()
 
     back = [steps.index(o) for o in range(1, visits)]
-    for o in range(1, visits):
+    for o in range(visits - 1, 0, -1):
         back_copy(o, own).start()
     fan_out(own)
     for n in units:

time: 31.3 us -> 30.8 us (0.984)
  Pallas kernels: 30.4 us -> 29.9 us
    pallas_call x1, Pallas kernels: 26.4 us -> 25.9 us  [coadds(): pl.pallas_call(functools.partial(coadd_kernel, chips, visits), in_specs=[...]
where the time goes in v8:
time: 30.8 us; the launch traced here: 30.6 us
  Pallas kernels  29.9 us (97%)
  between operations  0.69 us (2%)
    pallas_call x1, Pallas kernels, coadds(): pl.pallas_call(functools.partial(coadd_kernel, chips, visits), in_specs=[...  25.9 us
    pallas_call x1, Pallas kernels, subtract(): pl.pallas_call(functools.partial(match_kernel, kernel, group), in_specs=[...  4.02 us

profile of v8, /device:TPU:0, one launch (start us, length us, event | category | flops | bytes accessed | tf_op | source)
XLA Modules:
  0.0 30.6 jit_solution(15003960543849040196)
XLA Ops:
  0.6 0.0 copy-start.2
  0.6 0.0 copy-start
  0.7 0.0 copy-start.1
  0.7 25.9 %coadds.1 = bf16[4,2,256,256]{3,2,1,0:T(8,128)(2,1)S(1)} custom-call(s32[1,32]{1,0:T(1,128)} %bitcast.7, bf16[1,32]{1,0:T(2,128)(2,1)} %bitcast.9, bf16[32,256,256]{2,1,0:T(8,128)(2,1)} %tiles.3), custom_call_target="tpu_custom_call" | custom-call | tf_op jit(solution)/shard_map/coadds/pallas_call | solution.py:290
  26.6 0.0 copy-done.2
  26.6 0.0 copy-done
  26.6 0.0 copy-done.1
  26.6 4.0 %subtract.1 = (bf16[32,256,256]{2,1,0:T(8,128)(2,1)}, bf16[1,256,256]{2,1,0:T(8,128)(2,1)}) custom-call(s32[32]{0:T(128)S(1)} %bitcast.8, bf16[15,2,32]{2,1,0:T(2,128)(2,1)S(1)} %bitcast.6, bf16[32,256,256]{2,1,0:T(8,128)(2,1)S(1)} %copy-done, bf16[8,256,256]{2,1,0:T(8,128)(2,1)S(1)} %bitcast.5), custom_call_target="tpu_custom_call" | custom-call | tf_op jit(solution)/shard_map/subtract/pallas_call | solution.py:380
Async XLA Ops:
  0.6 26.0 %copy-start.2 = (s32[32,1]{0,1:T(1,128)S(1)}, s32[32,1]{0,1:T(1,128)}, u32[]{:S(2)}) copy-start(s32[32,1]{0,1:T(1,128)} %param.7) | copy-start | bytes 388
  0.6 26.0 %copy-start = (bf16[32,256,256]{2,1,0:T(8,128)(2,1)S(1)}, bf16[32,256,256]{2,1,0:T(8,128)(2,1)}, u32[]{:S(2)}) copy-start(bf16[32,256,256]{2,1,0:T(8,128)(2,1)} %tiles.3) | copy-start | bytes 12582916
  0.7 26.0 %copy-start.1 = (bf16[32,2,15]{0,1,2:T(2,128)(2,1)S(1)}, bf16[32,2,15]{0,1,2:T(2,128)(2,1)}, u32[]{:S(2)}) copy-start(bf16[32,2,15]{0,1,2:T(2,128)(2,1)} %param.6) | copy-start | bytes 5764
